TPU v7x, 32 devices: a whole 2x2x4 slice. The times are simulated.
32 devices in a mesh: grp: 4 (over y, x), ctx: 8 (over z, core).
Axes of the slice: x: 2, y: 2, z: 4, core: 2. Of those that a mesh axis runs over, the one named last changes fastest.
Arguments:
- queries: bfloat16 [4096, 2048], P(('grp', 'ctx')), parts along dimension 0, may hold values from -80 to 80
- keys: bfloat16 [4096, 512], P(('grp', 'ctx')), parts along dimension 0, may hold values from -4 to 4
- values: bfloat16 [4096, 512], P(('grp', 'ctx')), parts along dimension 0, may hold values from -6 to 6
- doc_lengths: int32 [32], P('grp'), parts along dimension 0, may hold values from 1 to 256, 1024 in all
- loader_pos: int32 [4096], P(('grp', 'ctx')), parts along dimension 0, may hold values from 0 to 1023, as said below
Outputs:
- attended: bfloat16 [4096, 2048], P(('grp', 'ctx')), parts along dimension 0
There are 4 independent parts, one for each index of `grp`. A program takes and returns all parts, laid end to end along the dimension named above; each array names one. Nothing has to cross between parts.
Inputs may be any that keep to these rules, and one draw needn't show every extreme that they name: loader_pos is a permutation of the packed positions; each block of 128 rows of it holds exactly 16 positions of every block of 128 consecutive packed positions.
All inputs are finite; a program needn't handle non-finite values.
Results may differ from a plain program's by a relative error of at most 0.0033.
Values may be sent and summed in bfloat16 or wider, within the bound.
No kernel may reach another device: no remote copies, remote signals or barrier semaphores. Data moves between devices by JAX's collectives and lax.ppermute only.
A program may use at most 64 MiB of HBM per device.

v0:
```python
import jax
import jax.numpy as jnp
from jax import lax
from jax.sharding import PartitionSpec as P

KEY_VALUE_HEADS = 4
HEAD_WIDTH = 128
REACH = 2


masked_value = -1e30


def shifted(block, axis, distance):
    devices = range(lax.axis_size(axis))
    route = [(i - distance, i) for i in devices if i - distance in devices]
    return lax.ppermute(block, axis, route)


def doc_index(positions, ends):
    return jnp.sum((positions[:, None] >= ends[None, :]).astype(jnp.int32), axis=1)


def attend(query_rows, k_win, v_win, q_pos, k_pos, ends):
    routed_rows = query_rows.shape[0]
    query_group = query_rows.shape[1] // (KEY_VALUE_HEADS * HEAD_WIDTH)
    q_doc = doc_index(q_pos, ends)
    k_doc = doc_index(k_pos, ends)
    allowed = (
        (k_pos[None, :] <= q_pos[:, None])
        & (q_doc[:, None] == k_doc[None, :])
        & (k_pos[None, :] >= 0)
    )
    query_head_rows = query_rows.reshape(routed_rows, KEY_VALUE_HEADS, query_group, HEAD_WIDTH)
    results = []
    for head_number in range(KEY_VALUE_HEADS):
        k_part = k_win[:, head_number * HEAD_WIDTH : (head_number + 1) * HEAD_WIDTH]
        v_part = v_win[:, head_number * HEAD_WIDTH : (head_number + 1) * HEAD_WIDTH]
        scores = jnp.einsum(
            "tgd,wd->gtw",
            query_head_rows[:, head_number],
            k_part,
            preferred_element_type=jnp.float32,
        ) * (1.0 / HEAD_WIDTH**0.5)
        scores = jnp.where(allowed[None], scores, masked_value)
        top = jnp.max(scores, axis=-1, keepdims=True)
        weight = jnp.exp(scores - top)
        total = jnp.sum(weight, axis=-1, keepdims=True)
        rounded = weight.astype(jnp.bfloat16)
        mixed = jnp.einsum(
            "gtw,wd->tgd", rounded, v_part, preferred_element_type=jnp.float32
        ) / jnp.transpose(total, (1, 0, 2))
        results.append(mixed.reshape(routed_rows, query_group * HEAD_WIDTH))
    return jnp.concatenate(results, axis=1).astype(jnp.bfloat16)


def on_device(queries, keys, values, doc_lengths, loader_pos):
    routed_rows = queries.shape[0]
    shards = lax.axis_size("ctx")
    cap_rows = routed_rows // shards
    shard_index = lax.axis_index("ctx")
    first_row = shard_index * routed_rows
    window = (REACH + 1) * routed_rows
    order = jnp.argsort(loader_pos)
    send_q = queries[order].reshape(shards, cap_rows, -1)
    send_k = keys[order].reshape(shards, cap_rows, -1)
    send_v = values[order].reshape(shards, cap_rows, -1)
    send_pos = loader_pos[order].reshape(shards, cap_rows)
    got_q, got_k, got_v, got_pos = (
        lax.all_to_all(send_q, "ctx", split_axis=0, concat_axis=0, tiled=True),
        lax.all_to_all(send_k, "ctx", split_axis=0, concat_axis=0, tiled=True),
        lax.all_to_all(send_v, "ctx", split_axis=0, concat_axis=0, tiled=True),
        lax.all_to_all(send_pos, "ctx", split_axis=0, concat_axis=0, tiled=True),
    )
    local = (got_pos.reshape(-1) - first_row).astype(jnp.int32)
    place = jnp.argsort(local)
    own_q = got_q.reshape(routed_rows, -1)[place]
    own_k = got_k.reshape(routed_rows, -1)[place]
    own_v = got_v.reshape(routed_rows, -1)[place]
    pieces_k = []
    pieces_v = []
    for step in range(REACH, 0, -1):
        far_k, far_v = shifted((own_k, own_v), "ctx", step)
        pieces_k.append(far_k)
        pieces_v.append(far_v)
    win_k = jnp.concatenate(pieces_k + [own_k], axis=0)
    win_v = jnp.concatenate(pieces_v + [own_v], axis=0)
    ends = jnp.cumsum(doc_lengths)
    q_pos = first_row + jnp.arange(routed_rows, dtype=jnp.int32)
    k_pos = first_row - REACH * routed_rows + jnp.arange(window, dtype=jnp.int32)
    packed_out = attend(own_q, win_k, win_v, q_pos, k_pos, ends)
    outgoing = packed_out[local].reshape(shards, cap_rows, -1)
    returned = lax.all_to_all(outgoing, "ctx", split_axis=0, concat_axis=0, tiled=True).reshape(
        routed_rows, -1
    )
    return returned[jnp.argsort(order)]


def solution(mesh):
    placed = (
        P(("grp", "ctx"), None),
        P(("grp", "ctx"), None),
        P(("grp", "ctx"), None),
        P("grp"),
        P(("grp", "ctx")),
    )
    return jax.shard_map(
        on_device, mesh=mesh, in_specs=placed, out_specs=P(("grp", "ctx"), None), check_vma=False
    )
```

profile of v0, /device:TPU:0, one launch (start us, length us, event | category | flops | bytes accessed | tf_op | source)
XLA Modules:
  0.0 94.2 jit_solution(3439213731322221824)
XLA Ops:
  0.0 0.7 copy-done.1
  0.7 2.5 %sort.45 = (s32[128]{0:T(128)}, s32[128]{0:T(128)S(1)}) sort(s32[128]{0:T(128)S(1)} %copy-done.1, s32[128]{0:T(128)S(1)} %iota.24), dimensions={0}, to_apply=%region_0.0 | sort | flops 896 | bytes 2048 | tf_op jit(solution)/shard_map/jit(argsort)/sort | solution.py:64
  3.8 1.2 %gather_fusion.1 = s32[128]{0:T(128)S(1)} fusion(s32[128]{0:T(128)S(1)} %copy-done.1, s32[1024]{0:T(1024)S(1)} %pad_clamp_fusion.3), kind=kCustom, calls=%fused_computation.1 | custom fusion | bytes 1536 | tf_op jit(solution)/shard_map/gather | solution.py:68
  5.1 0.7 all_to_all.19
  5.8 6.3 %all-to-all-start.1 = ((s32[8,1,16]{2,1,0:T(1,128)}), s32[8,1,16]{2,1,0:T(1,128)S(1)}, u32[]{:S(2)}, u32[]{:S(2)}) async-start(s32[8,1,16]{2,1,0:T(1,128)} %bitcast.2), calls=%async_computation.1 | async-start | bytes 8192 | tf_op jit(solution)/shard_map/all_to_all | solution.py:73
  12.1 1.5 %gather_fusion.3 = bf16[128,512]{1,0:T(8,128)(2,1)} fusion(bf16[128,512]{1,0:T(8,128)(2,1)S(1)} %copy-done.2, s32[1024]{0:T(1024)S(1)} %pad_clamp_fusion.3), kind=kCustom, calls=%fused_computation.3 | custom fusion | bytes 262656 | tf_op jit(solution)/shard_map/gather | solution.py:66
  13.6 4.0 %all-to-all-done.1 = s32[8,1,16]{2,1,0:T(1,128)S(1)} async-done(((s32[8,1,16]{2,1,0:T(1,128)}), s32[8,1,16]{2,1,0:T(1,128)S(1)}, u32[]{:S(2)}, u32[]{:S(2)}) %all-to-all-start.1) | async-done | bytes 544 | tf_op jit(solution)/shard_map/all_to_all | solution.py:73
  17.6 3.5 %all-to-all-start.2 = ((bf16[8,16,512]{2,1,0:T(8,128)(2,1)}), bf16[8,16,512]{2,1,0:T(8,128)(2,1)S(1)}, u32[]{:S(2)}, u32[]{:S(2)}) async-start(bf16[8,16,512]{2,1,0:T(8,128)(2,1)} %bitcast.6), calls=%async_computation.2 | async-start | bytes 262144 | tf_op jit(solution)/shard_map/all_to_all | solution.py:71
  21.2 1.5 %gather_fusion = bf16[128,512]{1,0:T(8,128)(2,1)} fusion(bf16[128,512]{1,0:T(8,128)(2,1)S(1)} %copy-done.3, s32[1024]{0:T(1024)S(1)} %pad_clamp_fusion.3), kind=kCustom, calls=%fused_computation | custom fusion | bytes 262656 | tf_op jit(solution)/shard_map/gather | solution.py:67
  23.7 4.2 %all-to-all-done.2 = bf16[8,16,512]{2,1,0:T(8,128)(2,1)S(1)} async-done(((bf16[8,16,512]{2,1,0:T(8,128)(2,1)}), bf16[8,16,512]{2,1,0:T(8,128)(2,1)S(1)}, u32[]{:S(2)}, u32[]{:S(2)}) %all-to-all-start.2) | async-done | bytes 131104 | tf_op jit(solution)/shard_map/all_to_all | solution.py:71
  27.9 3.4 %all-to-all-start = ((bf16[8,16,512]{2,1,0:T(8,128)(2,1)}), bf16[8,16,512]{2,1,0:T(8,128)(2,1)S(1)}, u32[]{:S(2)}, u32[]{:S(2)}) async-start(bf16[8,16,512]{2,1,0:T(8,128)(2,1)} %bitcast), calls=%async_computation | async-start | bytes 262144 | tf_op jit(solution)/shard_map/all_to_all | solution.py:72
  31.5 1.7 %gather_fusion.5 = bf16[128,2048]{1,0:T(8,128)(2,1)} fusion(bf16[128,2048]{1,0:T(8,128)(2,1)S(1)} %copy-done, s32[1024]{0:T(1024)S(1)} %pad_clamp_fusion.3), kind=kCustom, calls=%fused_computation.5 | custom fusion | bytes 1049088 | tf_op jit(solution)/shard_map/gather | solution.py:65
  34.4 2.5 %sort.46 = (s32[128]{0:T(128)}, s32[128]{0:T(128)S(1)}) sort(s32[128]{0:T(128)S(1)} %sub.58, s32[128]{0:T(128)S(1)} %iota.25), dimensions={0}, to_apply=%region_1.2 | sort | flops 896 | bytes 2048 | tf_op jit(solution)/shard_map/jit(argsort)/sort | solution.py:76
  36.9 1.1 %all-to-all-done = bf16[8,16,512]{2,1,0:T(8,128)(2,1)S(1)} async-done(((bf16[8,16,512]{2,1,0:T(8,128)(2,1)}), bf16[8,16,512]{2,1,0:T(8,128)(2,1)S(1)}, u32[]{:S(2)}, u32[]{:S(2)}) %all-to-all-start) | async-done | bytes 131104 | tf_op jit(solution)/shard_map/all_to_all | solution.py:72
  38.0 4.0 %all-to-all-start.3 = ((bf16[8,16,2048]{2,1,0:T(8,128)(2,1)}), bf16[8,16,2048]{2,1,0:T(8,128)(2,1)S(1)}, u32[]{:S(2)}, u32[]{:S(2)}) async-start(bf16[8,16,2048]{2,1,0:T(8,128)(2,1)} %bitcast.9), calls=%async_computation.3 | async-start | bytes 1048576 | tf_op jit(solution)/shard_map/all_to_all | solution.py:70
  42.0 0.8 gather_fusion.4
  42.9 3.9 %collective-permute-start.2 = (bf16[128,512]{1,0:T(8,128)(2,1)S(1)}, bf16[128,512]{1,0:T(8,128)(2,1)S(1)}, u32[]{:S(2)}, u32[]{:S(2)}) collective-permute-start(bf16[128,512]{1,0:T(8,128)(2,1)S(1)} %gather_fusion.4), channel_id=1, source_target_pairs={{0,2},{1,3},{2,4},{3,5},{4,6},{5,7},{8,10},{9,11},{10,12},{11,13},... | collective-permute-start | bytes 393224 | tf_op jit(solution)/shard_map/ppermute | solution.py:17
  46.8 1.8 %collective-permute-start.3 = (bf16[128,512]{1,0:T(8,128)(2,1)S(1)}, bf16[128,512]{1,0:T(8,128)(2,1)S(1)}, u32[]{:S(2)}, u32[]{:S(2)}) collective-permute-start(bf16[128,512]{1,0:T(8,128)(2,1)S(1)} %gather_fusion.4), channel_id=1, source_target_pairs={{0,1},{1,2},{2,3},{3,4},{4,5},{5,6},{6,7},{8,9},{9,10},{10,11},{11... | collective-permute-start | bytes 393224 | tf_op jit(solution)/shard_map/ppermute | solution.py:17
  48.6 0.8 gather_fusion.2
  49.6 3.5 %collective-permute-start = (bf16[128,512]{0,1:T(8,128)(2,1)S(1)}, bf16[128,512]{0,1:T(8,128)(2,1)S(1)}, u32[]{:S(2)}, u32[]{:S(2)}) collective-permute-start(bf16[128,512]{0,1:T(8,128)(2,1)S(1)} %copy.51), channel_id=1, source_target_pairs={{0,2},{1,3},{2,4},{3,5},{4,6},{5,7},{8,10},{9,11},{10,12},{11,13},... | collective-permute-start | bytes 393224 | tf_op jit(solution)/shard_map/ppermute | solution.py:17
  53.1 3.2 %collective-permute-start.1 = (bf16[128,512]{0,1:T(8,128)(2,1)S(1)}, bf16[128,512]{0,1:T(8,128)(2,1)S(1)}, u32[]{:S(2)}, u32[]{:S(2)}) collective-permute-start(bf16[128,512]{0,1:T(8,128)(2,1)S(1)} %copy.51), channel_id=1, source_target_pairs={{0,1},{1,2},{2,3},{3,4},{4,5},{5,6},{6,7},{8,9},{9,10},{10,11},{11... | collective-permute-start | bytes 393224 | tf_op jit(solution)/shard_map/ppermute | solution.py:17
  56.4 0.8 collective-permute-done
  57.3 0.8 pad_maximum_fusion.1
  58.1 0.9 gather_fusion.6
  59.8 1.1 %fusion.35 = (f32[4,128]{1,0:T(4,128)S(1)}, f32[4,128,384]{1,2,0:T(8,128)S(1)}) fusion(bf16[128,4,4,128]{0,3,2,1:T(8,128)(2,1)S(1)} %bitcast.141, bf16[384,512]{1,0:T(8,128)(2,1)} %copy-done.5, pred[128,384]{0,1:T(8,128)(4,1)S(1)} %and_and_fusion), kind=kOutput, calls=%fused_computation.84 | convolution fusion | flops 50920960 | bytes 1067008 | tf_op jit(solution)/shard_map/tgd,wd->gtw/dot_general | solution.py:39
  61.0 1.1 %fusion.34 = (f32[4,128]{1,0:T(4,128)S(1)}, f32[4,128,384]{1,2,0:T(8,128)S(1)}) fusion(bf16[128,4,4,128]{0,3,2,1:T(8,128)(2,1)S(1)} %bitcast.142, bf16[384,512]{1,0:T(8,128)(2,1)} %copy-done.5, pred[128,384]{0,1:T(8,128)(4,1)S(1)} %and_and_fusion), kind=kOutput, calls=%fused_computation.83 | convolution fusion | flops 50920960 | bytes 1067008 | tf_op jit(solution)/shard_map/tgd,wd->gtw/dot_general | solution.py:39
  62.3 0.9 copy-done.4
  65.2 1.7 %gather_fusion.7 = bf16[128,2048]{1,0:T(8,128)(2,1)} fusion(bf16[128,2048]{1,0:T(8,128)(2,1)S(1)} %pad_maximum_fusion, s32[1024]{0:T(1024)S(1)} %pad_clamp_fusion.1), kind=kCustom, calls=%fused_computation.7 | custom fusion | bytes 1049088 | tf_op jit(solution)/shard_map/gather | solution.py:92
  67.0 10.1 %all-to-all-start.4 = ((bf16[8,16,2048]{2,1,0:T(8,128)(2,1)}), bf16[8,16,2048]{2,1,0:T(8,128)(2,1)S(1)}, u32[]{:S(2)}, u32[]{:S(2)}) async-start(bf16[8,16,2048]{2,1,0:T(8,128)(2,1)} %bitcast.47), calls=%async_computation.4 | async-start | bytes 1048576 | tf_op jit(solution)/shard_map/all_to_all | solution.py:93
  77.8 2.6 %sort.47 = (s32[128]{0:T(128)}, s32[128]{0:T(128)S(1)}) sort(s32[128]{0:T(128)S(1)} %copy-done.8, s32[128]{0:T(128)S(1)} %iota.28), dimensions={0}, to_apply=%region_13.14 | sort | flops 896 | bytes 2048 | tf_op jit(solution)/shard_map/jit(argsort)/sort | solution.py:96
  80.4 12.1 %all-to-all-done.4 = bf16[8,16,2048]{2,1,0:T(8,128)(2,1)S(1)} async-done(((bf16[8,16,2048]{2,1,0:T(8,128)(2,1)}), bf16[8,16,2048]{2,1,0:T(8,128)(2,1)S(1)}, u32[]{:S(2)}, u32[]{:S(2)}) %all-to-all-start.4) | async-done | bytes 524320 | tf_op jit(solution)/shard_map/all_to_all | solution.py:93
  92.5 1.7 %gather_fusion.8 = bf16[128,2048]{1,0:T(8,128)(2,1)} fusion(bf16[128,2048]{1,0:T(8,128)(2,1)S(1)} %bitcast.136, s32[1024]{0:T(1024)S(1)} %pad_clamp_fusion), kind=kCustom, calls=%fused_computation.8 | custom fusion | bytes 1049088 | tf_op jit(solution)/shard_map/gather | solution.py:96
  (62 shorter events, 6.9 us)
Async XLA Ops:
  0.0 31.5 %copy-start = (bf16[128,2048]{1,0:T(8,128)(2,1)S(1)}, bf16[128,2048]{1,0:T(8,128)(2,1)}, u32[]{:S(2)}) copy-start(bf16[128,2048]{1,0:T(8,128)(2,1)} %param.5) | copy-start | bytes 1572868
  0.0 0.7 copy-start.1
  3.3 0.6 copy-start.7
  3.8 8.3 %copy-start.2 = (bf16[128,512]{1,0:T(8,128)(2,1)S(1)}, bf16[128,512]{1,0:T(8,128)(2,1)}, u32[]{:S(2)}) copy-start(bf16[128,512]{1,0:T(8,128)(2,1)} %param.6) | copy-start | bytes 393220
  5.8 11.9 %all-to-all-start.1 = ((s32[8,1,16]{2,1,0:T(1,128)}), s32[8,1,16]{2,1,0:T(1,128)S(1)}, u32[]{:S(2)}, u32[]{:S(2)}) async-start(s32[8,1,16]{2,1,0:T(1,128)} %bitcast.2), calls=%async_computation.1 | async-start | bytes 8192 | tf_op jit(solution)/shard_map/all_to_all | solution.py:73
  17.6 3.5 %copy-start.3 = (bf16[128,512]{1,0:T(8,128)(2,1)S(1)}, bf16[128,512]{1,0:T(8,128)(2,1)}, u32[]{:S(2)}) copy-start(bf16[128,512]{1,0:T(8,128)(2,1)} %param.7) | copy-start | bytes 393220
  17.6 10.2 %all-to-all-start.2 = ((bf16[8,16,512]{2,1,0:T(8,128)(2,1)}), bf16[8,16,512]{2,1,0:T(8,128)(2,1)S(1)}, u32[]{:S(2)}, u32[]{:S(2)}) async-start(bf16[8,16,512]{2,1,0:T(8,128)(2,1)} %bitcast.6), calls=%async_computation.2 | async-start | bytes 262144 | tf_op jit(solution)/shard_map/all_to_all | solution.py:71
  22.7 0.7 copy-start.6
  27.9 10.1 %all-to-all-start = ((bf16[8,16,512]{2,1,0:T(8,128)(2,1)}), bf16[8,16,512]{2,1,0:T(8,128)(2,1)S(1)}, u32[]{:S(2)}, u32[]{:S(2)}) async-start(bf16[8,16,512]{2,1,0:T(8,128)(2,1)} %bitcast), calls=%async_computation | async-start | bytes 262144 | tf_op jit(solution)/shard_map/all_to_all | solution.py:72
  38.0 20.1 %all-to-all-start.3 = ((bf16[8,16,2048]{2,1,0:T(8,128)(2,1)}), bf16[8,16,2048]{2,1,0:T(8,128)(2,1)S(1)}, u32[]{:S(2)}, u32[]{:S(2)}) async-start(bf16[8,16,2048]{2,1,0:T(8,128)(2,1)} %bitcast.9), calls=%async_computation.3 | async-start | bytes 1048576 | tf_op jit(solution)/shard_map/all_to_all | solution.py:70
  42.9 13.5 %collective-permute-start.2 = (bf16[128,512]{1,0:T(8,128)(2,1)S(1)}, bf16[128,512]{1,0:T(8,128)(2,1)S(1)}, u32[]{:S(2)}, u32[]{:S(2)}) collective-permute-start(bf16[128,512]{1,0:T(8,128)(2,1)S(1)} %gather_fusion.4), channel_id=1, source_target_pairs={{0,2},{1,3},{2,4},{3,5},{4,6},{5,7},{8,10},{9,11},{10,12},{11,13},... | collective-permute-start | bytes 393224 | tf_op jit(solution)/shard_map/ppermute | solution.py:17
  46.8 9.5 %collective-permute-start.3 = (bf16[128,512]{1,0:T(8,128)(2,1)S(1)}, bf16[128,512]{1,0:T(8,128)(2,1)S(1)}, u32[]{:S(2)}, u32[]{:S(2)}) collective-permute-start(bf16[128,512]{1,0:T(8,128)(2,1)S(1)} %gather_fusion.4), channel_id=1, source_target_pairs={{0,1},{1,2},{2,3},{3,4},{4,5},{5,6},{6,7},{8,9},{9,10},{10,11},{11... | collective-permute-start | bytes 393224 | tf_op jit(solution)/shard_map/ppermute | solution.py:17
  49.6 7.7 %collective-permute-start = (bf16[128,512]{0,1:T(8,128)(2,1)S(1)}, bf16[128,512]{0,1:T(8,128)(2,1)S(1)}, u32[]{:S(2)}, u32[]{:S(2)}) collective-permute-start(bf16[128,512]{0,1:T(8,128)(2,1)S(1)} %copy.51), channel_id=1, source_target_pairs={{0,2},{1,3},{2,4},{3,5},{4,6},{5,7},{8,10},{9,11},{10,12},{11,13},... | collective-permute-start | bytes 393224 | tf_op jit(solution)/shard_map/ppermute | solution.py:17
  53.1 4.2 %collective-permute-start.1 = (bf16[128,512]{0,1:T(8,128)(2,1)S(1)}, bf16[128,512]{0,1:T(8,128)(2,1)S(1)}, u32[]{:S(2)}, u32[]{:S(2)}) collective-permute-start(bf16[128,512]{0,1:T(8,128)(2,1)S(1)} %copy.51), channel_id=1, source_target_pairs={{0,1},{1,2},{2,3},{3,4},{4,5},{5,6},{6,7},{8,9},{9,10},{10,11},{11... | collective-permute-start | bytes 393224 | tf_op jit(solution)/shard_map/ppermute | solution.py:17
  56.4 3.2 %copy-start.5 = (bf16[384,512]{1,0:T(8,128)(2,1)}, bf16[384,512]{1,0:T(8,128)(2,1)S(1)}, u32[]{:S(2)}) copy-start(bf16[384,512]{1,0:T(8,128)(2,1)S(1)} %constant_dynamic-update-slice_fusion) | copy-start | bytes 1179652
  62.1 1.0 %copy-start.4 = (bf16[384,512]{0,1:T(8,128)(2,1)S(1)}, bf16[384,512]{0,1:T(8,128)(2,1)}, u32[]{:S(2)}) copy-start(bf16[384,512]{0,1:T(8,128)(2,1)} %pad_maximum_fusion.1) | copy-start | bytes 1179652
  67.0 25.5 %all-to-all-start.4 = ((bf16[8,16,2048]{2,1,0:T(8,128)(2,1)}), bf16[8,16,2048]{2,1,0:T(8,128)(2,1)S(1)}, u32[]{:S(2)}, u32[]{:S(2)}) async-start(bf16[8,16,2048]{2,1,0:T(8,128)(2,1)} %bitcast.47), calls=%async_computation.4 | async-start | bytes 1048576 | tf_op jit(solution)/shard_map/all_to_all | solution.py:93
  77.1 0.7 copy-start.8
where the time goes:
time: 94.9 us; the launch traced here: 94.2 us
  starting transfers between devices  39.7 us (42%)
  waiting for transfers between devices  22.2 us (23%)
  local copies, waits for them, and re-layouts  17.7 us (19%)
  other arithmetic  10.2 us (11%)
  matrix products  3.95 us (4%)
    ppermute x4, starting transfers between devices, shifted(): return lax.ppermute(block, axis, route)  12.4 us
    all_to_all x1, waiting for transfers between devices, on_device(): lax.all_to_all(outgoing, 'ctx', split_axis=0, concat_axis=0, tiled=True)  12.1 us
    all_to_all x1, starting transfers between devices, on_device(): lax.all_to_all(outgoing, 'ctx', split_axis=0, concat_axis=0, tiled=True)  10.1 us
    all_to_all x1, starting transfers between devices, on_device(): lax.all_to_all(send_pos, 'ctx', split_axis=0, concat_axis=0, tiled=True)  6.33 us
    all_to_all x1, waiting for transfers between devices, on_device(): lax.all_to_all(send_k, 'ctx', split_axis=0, concat_axis=0, tiled=True)  4.19 us
    all_to_all x1, waiting for transfers between devices, on_device(): lax.all_to_all(send_pos, 'ctx', split_axis=0, concat_axis=0, tiled=True)  4.02 us
    all_to_all x1, starting transfers between devices, on_device(): lax.all_to_all(send_q, 'ctx', split_axis=0, concat_axis=0, tiled=True)  3.98 us
    all_to_all x1, starting transfers between devices, on_device(): lax.all_to_all(send_k, 'ctx', split_axis=0, concat_axis=0, tiled=True)  3.5 us
  transfers between devices with their start and end apart: 9, of which 5 were waited for; matrix products, arithmetic and copies ran while one was open for 15% of the time, Pallas kernels for 0%

commit v1 on v0

--- a/solution.py
+++ b/solution.py
@@ -1,14 +1,18 @@
 import jax
 import jax.numpy as jnp
 from jax import lax
+from jax.experimental import pallas as pl
+from jax.experimental.pallas import tpu as pltpu
 from jax.sharding import PartitionSpec as P
 
 KEY_VALUE_HEADS = 4
 HEAD_WIDTH = 128
 REACH = 2
+GATHER_SHARDS = 8
 
 
 masked_value = -1e30
+EXP2_SCALE = 1.4426950408889634 / HEAD_WIDTH**0.5
 
 
 def shifted(block, axis, distance):
@@ -54,7 +58,7 @@
     return jnp.concatenate(results, axis=1).astype(jnp.bfloat16)
 
 
-def on_device(queries, keys, values, doc_lengths, loader_pos):
+def routed(queries, keys, values, doc_lengths, loader_pos):
     routed_rows = queries.shape[0]
     shards = lax.axis_size("ctx")
     cap_rows = routed_rows // shards
@@ -96,6 +100,84 @@
     return returned[jnp.argsort(order)]
 
 
+def gathered_kernel(shards, doc_ref, pos_ref, q_ref, *refs):
+    k_refs, v_refs = refs[:shards], refs[shards : 2 * shards]
+    out_ref, bias_ref = refs[2 * shards :]
+    rows = q_ref.shape[0]
+    group = q_ref.shape[1] // (KEY_VALUE_HEADS * HEAD_WIDTH)
+
+    own = pos_ref[0:1, :]
+    square = (rows, rows)
+    diagonal = lax.broadcasted_iota(jnp.int32, square, 0) == lax.broadcasted_iota(jnp.int32, square, 1)
+    q_pos = jnp.sum(jnp.where(diagonal, own, 0), axis=1, keepdims=True)
+
+    def next_doc(j, carry):
+        end, first = carry
+        end = end + doc_ref[j]
+        return end, jnp.where(q_pos >= end, end, first)
+
+    _, q_first = lax.fori_loop(
+        0, doc_ref.shape[0], next_doc, (jnp.int32(0), jnp.zeros_like(q_pos)), unroll=True
+    )
+    for s in range(shards):
+        k_pos = pos_ref[s : s + 1, :]
+        allowed = (k_pos <= q_pos) & (k_pos >= q_first)
+        bias_ref[:, s * rows : (s + 1) * rows] = jnp.where(allowed, 0.0, masked_value)
+
+    for head in range(KEY_VALUE_HEADS):
+        lanes = slice(head * HEAD_WIDTH, (head + 1) * HEAD_WIDTH)
+        k_part = jnp.concatenate([r[:, lanes] for r in k_refs], axis=0)
+        v_part = jnp.concatenate([r[:, lanes] for r in v_refs], axis=0)
+        for g in range(group):
+            at = (head * group + g) * HEAD_WIDTH
+            q_part = q_ref[:, at : at + HEAD_WIDTH]
+            scores = lax.dot_general(
+                q_part, k_part, (((1,), (1,)), ((), ())), preferred_element_type=jnp.float32
+            )
+            scores = scores + bias_ref[...]
+            top = jnp.max(scores, axis=1, keepdims=True)
+            weight = jnp.exp2((scores - top) * EXP2_SCALE)
+            total = jnp.sum(weight, axis=1, keepdims=True)
+            mixed = jnp.dot(weight.astype(jnp.bfloat16), v_part, preferred_element_type=jnp.float32)
+            out_ref[:, at : at + HEAD_WIDTH] = (mixed / total).astype(jnp.bfloat16)
+
+
+def gathered(queries, keys, values, doc_lengths, loader_pos):
+    shards = lax.axis_size("ctx")
+    rows = queries.shape[0]
+
+    def from_peer(x, distance):
+        return lax.ppermute(x, "ctx", [(i, i ^ distance) for i in range(shards)])
+
+    pos = loader_pos.reshape(1, rows)
+    ks, vs = {0: keys}, {0: values}
+    for far in range(2, shards, 2):
+        ks[far], vs[far] = from_peer(keys, far), from_peer(values, far)
+    for near in range(0, shards, 2):
+        ks[near + 1], vs[near + 1] = from_peer(ks[near], 1), from_peer(vs[near], 1)
+    spread = lax.all_to_all(
+        jnp.broadcast_to(pos, (shards, rows)), "ctx", split_axis=0, concat_axis=0, tiled=True
+    )
+    me = lax.axis_index("ctx")
+    poss = spread[me ^ jnp.arange(shards)]
+    vmem = pl.BlockSpec(memory_space=pltpu.VMEM)
+    return pl.pallas_call(
+        lambda *refs: gathered_kernel(shards, *refs),
+        out_shape=jax.ShapeDtypeStruct(queries.shape, jnp.bfloat16),
+        in_specs=[pl.BlockSpec(memory_space=pltpu.SMEM)] + [vmem] * (2 + 2 * shards),
+        out_specs=vmem,
+        scratch_shapes=[pltpu.VMEM((rows, shards * rows), jnp.float32)],
+        compiler_params=pltpu.CompilerParams(vmem_limit_bytes=32 << 20),
+    )(doc_lengths, poss, queries, *[ks[s] for s in range(shards)], *[vs[s] for s in range(shards)])
+
+
+def on_device(queries, keys, values, doc_lengths, loader_pos):
+    shards = lax.axis_size("ctx")
+    if 2 <= shards <= GATHER_SHARDS and shards & (shards - 1) == 0:
+        return gathered(queries, keys, values, doc_lengths, loader_pos)
+    return routed(queries, keys, values, doc_lengths, loader_pos)
+
+
 def solution(mesh):
     placed = (
         P(("grp", "ctx"), None),

time: 94.9 us -> 41.9 us (0.44)
  starting transfers between devices: 39.7 us -> 21.3 us
  waiting for transfers between devices: 22.2 us -> 8.39 us
  local copies, waits for them, and re-layouts: 17.7 us -> 4.7 us
  other arithmetic: 10.2 us -> 0.01 us
  Pallas kernels: 0 us -> 7.09 us
  matrix products: 3.95 us -> 0 us
    all_to_all x5 -> x1, starting transfers between devices: 27.3 us -> 8.66 us  [gathered(): lax.all_to_all(jnp.broadcast_to(pos, (shards, rows)), 'ctx', split_axis=0...]
    all_to_all x5 -> x1, waiting for transfers between devices: 21.3 us -> 3.92 us  [gathered(): lax.all_to_all(jnp.broadcast_to(pos, (shards, rows)), 'ctx', split_axis=0...]
    gather x11 -> x1, local copies, waits for them, and re-layouts: 12.4 us -> 0.55 us  [gathered(): poss = spread[me ^ jnp.arange(shards)]]
    sort x3 -> x0, other arithmetic: 7.68 us -> none  [the longest x1 2.61 us: on_device(): return returned[jnp.argsort(order)]]
    pallas_call x0 -> x1, Pallas kernels: none -> 7.09 us  [gathered(): pl.pallas_call(lambda *refs: gathered_kernel(shards, *refs), out_shape=ja...]
    dot_general x8 -> x0, matrix products: 3.95 us -> none  [the longest x4 2.82 us: attend(): jnp.einsum('tgd,wd->gtw', query_head_rows[:, head_number], k_part, prefer...]
    ppermute x4 -> x14, waiting for transfers between devices: 0.88 us -> 4.47 us  [from_peer(): return lax.ppermute(x, 'ctx', [(i, i ^ distance) for i in range(shards)])]
    broadcast_in_dim x0 -> x1, local copies, waits for them, and re-layouts: none -> 1.25 us  [gathered(): jnp.broadcast_to(pos, (shards, rows))]
  transfers between devices with their start and end apart: 9 -> 15, of which waited for: 5 -> 2; matrix products, arithmetic and copies ran while one was open for 15% -> 4% of each run, Pallas kernels for 0% -> 0%
where the time goes in v1:
time: 41.9 us; the launch traced here: 41.6 us
  starting transfers between devices  21.3 us (51%)
  waiting for transfers between devices  8.39 us (20%)
  Pallas kernels  7.09 us (17%)
  local copies, waits for them, and re-layouts  4.7 us (11%)
    ppermute x14, starting transfers between devices, from_peer(): return lax.ppermute(x, 'ctx', [(i, i ^ distance) for i in range(shards)])  12.7 us
    all_to_all x1, starting transfers between devices, gathered(): lax.all_to_all(jnp.broadcast_to(pos, (shards, rows)), 'ctx', split_axis=0...  8.66 us
    pallas_call x1, Pallas kernels, gathered(): pl.pallas_call(lambda *refs: gathered_kernel(shards, *refs), out_shape=ja...  7.09 us
    ppermute x14, waiting for transfers between devices, from_peer(): return lax.ppermute(x, 'ctx', [(i, i ^ distance) for i in range(shards)])  4.47 us
    all_to_all x1, waiting for transfers between devices, gathered(): lax.all_to_all(jnp.broadcast_to(pos, (shards, rows)), 'ctx', split_axis=0...  3.92 us
    unnamed x8, local copies, waits for them, and re-layouts  2.89 us
    broadcast_in_dim x1, local copies, waits for them, and re-layouts, gathered(): jnp.broadcast_to(pos, (shards, rows))  1.25 us
  transfers between devices with their start and end apart: 15, of which 2 were waited for; matrix products, arithmetic and copies ran while one was open for 4% of the time, Pallas kernels for 0%

profile of v1, /device:TPU:0, one launch (start us, length us, event | category | flops | bytes accessed | tf_op | source)
XLA Modules:
  0.0 41.6 jit_solution(7057749919032503809)
XLA Ops:
  0.0 4.0 %collective-permute-start.3 = (bf16[128,512]{1,0:T(8,128)(2,1)}, bf16[128,512]{1,0:T(8,128)(2,1)S(1)}, u32[]{:S(2)}, u32[]{:S(2)}) collective-permute-start(bf16[128,512]{1,0:T(8,128)(2,1)} %refs_3_.1), channel_id=1, source_target_pairs={{0,4},{1,5},{2,6},{3,7},{4,0},{5,1},{6,2},{7,3},{8,12},{9,13},{10,... | collective-permute-start | bytes 393224 | tf_op jit(solution)/shard_map/ppermute | solution.py:150
  4.0 1.6 %collective-permute-start.1 = (bf16[128,512]{1,0:T(8,128)(2,1)}, bf16[128,512]{1,0:T(8,128)(2,1)S(1)}, u32[]{:S(2)}, u32[]{:S(2)}) collective-permute-start(bf16[128,512]{1,0:T(8,128)(2,1)} %refs_3_.1), channel_id=1, source_target_pairs={{0,2},{1,3},{2,0},{3,1},{4,6},{5,7},{6,4},{7,5},{8,10},{9,11},{10,... | collective-permute-start | bytes 393224 | tf_op jit(solution)/shard_map/ppermute | solution.py:150
  5.6 0.0 collective-permute-start
  5.6 0.0 collective-permute-start.5
  5.6 1.9 %collective-permute-start.10 = (bf16[128,512]{1,0:T(8,128)(2,1)}, bf16[128,512]{1,0:T(8,128)(2,1)S(1)}, u32[]{:S(2)}, u32[]{:S(2)}) collective-permute-start(bf16[128,512]{1,0:T(8,128)(2,1)} %refs_11_.1), channel_id=1, source_target_pairs={{0,4},{1,5},{2,6},{3,7},{4,0},{5,1},{6,2},{7,3},{8,12},{9,13},{10,... | collective-permute-start | bytes 393224 | tf_op jit(solution)/shard_map/ppermute | solution.py:150
  7.5 4.4 %collective-permute-done.3.refs_7_ = bf16[128,512]{1,0:T(8,128)(2,1)S(1)} collective-permute-done((bf16[128,512]{1,0:T(8,128)(2,1)}, bf16[128,512]{1,0:T(8,128)(2,1)S(1)}, u32[]{:S(2)}, u32[]{:S(2)}) %collective-permute-start.3) | collective-permute-done | bytes 131104 | tf_op jit(solution)/shard_map/ppermute | solution.py:150
  12.0 0.4 %collective-permute-start.8 = (bf16[128,512]{1,0:T(8,128)(2,1)}, bf16[128,512]{1,0:T(8,128)(2,1)S(1)}, u32[]{:S(2)}, u32[]{:S(2)}) collective-permute-start(bf16[128,512]{1,0:T(8,128)(2,1)} %refs_11_.1), channel_id=1, source_target_pairs={{0,2},{1,3},{2,0},{3,1},{4,6},{5,7},{6,4},{7,5},{8,10},{9,11},{10,... | collective-permute-start | bytes 393224 | tf_op jit(solution)/shard_map/ppermute | solution.py:150
  12.4 0.0 collective-permute-done.1.refs_5_
  12.4 0.0 collective-permute-start.7
  12.4 0.0 collective-permute-done.refs_4_
  12.4 3.0 %collective-permute-start.12 = (bf16[128,512]{1,0:T(8,128)(2,1)}, bf16[128,512]{1,0:T(8,128)(2,1)S(1)}, u32[]{:S(2)}, u32[]{:S(2)}) collective-permute-start(bf16[128,512]{1,0:T(8,128)(2,1)} %refs_11_.1), channel_id=1, source_target_pairs={{0,6},{1,7},{2,4},{3,5},{4,2},{5,3},{6,0},{7,1},{8,14},{9,15},{10,... | collective-permute-start | bytes 393224 | tf_op jit(solution)/shard_map/ppermute | solution.py:150
  15.4 0.0 collective-permute-done.5.refs_9_
  15.4 0.2 collective-permute-start.4
  15.6 1.2 %broadcast_in_dim.2 = s32[8,1,128]{2,1,0:T(1,128)} broadcast(s32[128]{0:T(128)} %param.9), dimensions={2} | broadcast | bytes 4608 | tf_op jit(solution)/shard_map/broadcast_in_dim | solution.py:159
  16.9 8.7 %all-to-all-start = ((s32[8,1,128]{2,1,0:T(1,128)}), s32[8,1,128]{2,1,0:T(1,128)S(1)}, u32[]{:S(2)}, u32[]{:S(2)}) async-start(s32[8,1,128]{2,1,0:T(1,128)} %broadcast_in_dim.2), calls=%async_computation | async-start | bytes 8192 | tf_op jit(solution)/shard_map/all_to_all | solution.py:158
  25.5 0.5 %collective-permute-start.2 = (bf16[128,512]{1,0:T(8,128)(2,1)S(1)}, bf16[128,512]{1,0:T(8,128)(2,1)S(1)}, u32[]{:S(2)}, u32[]{:S(2)}) collective-permute-start(bf16[128,512]{1,0:T(8,128)(2,1)S(1)} %collective-permute-done.1.refs_5_), channel_id=1, source_target_pairs={{0,1},{1,0},{2,3},{3,2},{4,5},{5,4},{6,7},{7,6},{8,9},{9,8},{10,11... | collective-permute-start | bytes 393224 | tf_op jit(solution)/shard_map/ppermute | solution.py:150
  26.0 0.0 collective-permute-done.8.refs_13_
  26.0 0.1 collective-permute-start.6
  26.1 0.0 collective-permute-done.7.refs_12_
  26.1 0.4 %collective-permute-start.11 = (bf16[128,512]{1,0:T(8,128)(2,1)S(1)}, bf16[128,512]{1,0:T(8,128)(2,1)S(1)}, u32[]{:S(2)}, u32[]{:S(2)}) collective-permute-start(bf16[128,512]{1,0:T(8,128)(2,1)S(1)} %collective-permute-done.10.refs_15_), channel_id=1, source_target_pairs={{0,1},{1,0},{2,3},{3,2},{4,5},{5,4},{6,7},{7,6},{8,9},{9,8},{10,11... | collective-permute-start | bytes 393224 | tf_op jit(solution)/shard_map/ppermute | solution.py:150
  26.5 0.0 collective-permute-done.12.refs_17_
  26.5 0.1 collective-permute-start.9
  26.6 0.0 collective-permute-done.4.refs_8_
  26.6 0.4 %collective-permute-start.13 = (bf16[128,512]{1,0:T(8,128)(2,1)S(1)}, bf16[128,512]{1,0:T(8,128)(2,1)S(1)}, u32[]{:S(2)}, u32[]{:S(2)}) collective-permute-start(bf16[128,512]{1,0:T(8,128)(2,1)S(1)} %collective-permute-done.12.refs_17_), channel_id=1, source_target_pairs={{0,1},{1,0},{2,3},{3,2},{4,5},{5,4},{6,7},{7,6},{8,9},{9,8},{10,11... | collective-permute-start | bytes 393224 | tf_op jit(solution)/shard_map/ppermute | solution.py:150
  27.1 3.9 %all-to-all-done = s32[8,1,128]{2,1,0:T(1,128)S(1)} async-done(((s32[8,1,128]{2,1,0:T(1,128)}), s32[8,1,128]{2,1,0:T(1,128)S(1)}, u32[]{:S(2)}, u32[]{:S(2)}) %all-to-all-start) | async-done | bytes 4128 | tf_op jit(solution)/shard_map/all_to_all | solution.py:158
  31.0 0.6 %gather_fusion = s32[8,128]{1,0:T(8,128)S(1)} fusion(s32[8,128]{1,0:T(8,128)S(1)} %bitcast.3, s32[1024]{0:T(1024)S(1)} %pad_clamp_fusion), kind=kCustom, calls=%fused_computation | custom fusion | bytes 8224 | tf_op jit(solution)/shard_map/gather | solution.py:162
  31.6 0.0 collective-permute-done.6.refs_10_
  31.6 0.0 copy-done.3
  31.7 1.0 %copy-done = bf16[128,2048]{1,0:T(8,128)(2,1)S(1)} copy-done((bf16[128,2048]{1,0:T(8,128)(2,1)S(1)}, bf16[128,2048]{1,0:T(8,128)(2,1)}, u32[]{:S(2)}) %copy-start) | copy-done | bytes 524312
  32.7 0.9 %copy-done.1 = bf16[128,512]{1,0:T(8,128)(2,1)S(1)} copy-done((bf16[128,512]{1,0:T(8,128)(2,1)S(1)}, bf16[128,512]{1,0:T(8,128)(2,1)}, u32[]{:S(2)}) %copy-start.1) | copy-done | bytes 131096
  33.6 0.9 %copy-done.2 = bf16[128,512]{1,0:T(8,128)(2,1)S(1)} copy-done((bf16[128,512]{1,0:T(8,128)(2,1)S(1)}, bf16[128,512]{1,0:T(8,128)(2,1)}, u32[]{:S(2)}) %copy-start.2) | copy-done | bytes 131096
  34.5 7.1 %shard_map.55 = bf16[128,2048]{1,0:T(8,128)(2,1)} custom-call(s32[8]{0:T(128)S(1)} %copy-done.3, s32[8,128]{1,0:T(8,128)S(1)} %gather_fusion, bf16[128,2048]{1,0:T(8,128)(2,1)S(1)} %copy-done, bf16[128,512]{1,0:T(8,128)(2,1)S(1)} %copy-done.1, bf16[128,512]{1,0:T(8,128)(2,1)S(1)} %collective-permute-done.refs_4_, ...), custom_call_target="tpu_custom_call" | custom-call | tf_op jit(solution)/shard_map/pallas_call | solution.py:164
  (11 shorter events, 0.0 us)
Async XLA Ops:
  0.0 12.0 %collective-permute-start.3 = (bf16[128,512]{1,0:T(8,128)(2,1)}, bf16[128,512]{1,0:T(8,128)(2,1)S(1)}, u32[]{:S(2)}, u32[]{:S(2)}) collective-permute-start(bf16[128,512]{1,0:T(8,128)(2,1)} %refs_3_.1), channel_id=1, source_target_pairs={{0,4},{1,5},{2,6},{3,7},{4,0},{5,1},{6,2},{7,3},{8,12},{9,13},{10,... | collective-permute-start | bytes 393224 | tf_op jit(solution)/shard_map/ppermute | solution.py:150
  4.0 8.3 %collective-permute-start.1 = (bf16[128,512]{1,0:T(8,128)(2,1)}, bf16[128,512]{1,0:T(8,128)(2,1)S(1)}, u32[]{:S(2)}, u32[]{:S(2)}) collective-permute-start(bf16[128,512]{1,0:T(8,128)(2,1)} %refs_3_.1), channel_id=1, source_target_pairs={{0,2},{1,3},{2,0},{3,1},{4,6},{5,7},{6,4},{7,5},{8,10},{9,11},{10,... | collective-permute-start | bytes 393224 | tf_op jit(solution)/shard_map/ppermute | solution.py:150
  5.6 6.8 %collective-permute-start = (bf16[128,512]{1,0:T(8,128)(2,1)}, bf16[128,512]{1,0:T(8,128)(2,1)S(1)}, u32[]{:S(2)}, u32[]{:S(2)}) collective-permute-start(bf16[128,512]{1,0:T(8,128)(2,1)} %refs_3_.1), channel_id=1, source_target_pairs={{0,1},{1,0},{2,3},{3,2},{4,5},{5,4},{6,7},{7,6},{8,9},{9,8},{10,11... | collective-permute-start | bytes 393224 | tf_op jit(solution)/shard_map/ppermute | solution.py:150
  5.6 9.8 %collective-permute-start.5 = (bf16[128,512]{1,0:T(8,128)(2,1)}, bf16[128,512]{1,0:T(8,128)(2,1)S(1)}, u32[]{:S(2)}, u32[]{:S(2)}) collective-permute-start(bf16[128,512]{1,0:T(8,128)(2,1)} %refs_3_.1), channel_id=1, source_target_pairs={{0,6},{1,7},{2,4},{3,5},{4,2},{5,3},{6,0},{7,1},{8,14},{9,15},{10,... | collective-permute-start | bytes 393224 | tf_op jit(solution)/shard_map/ppermute | solution.py:150
  5.6 19.9 %collective-permute-start.10 = (bf16[128,512]{1,0:T(8,128)(2,1)}, bf16[128,512]{1,0:T(8,128)(2,1)S(1)}, u32[]{:S(2)}, u32[]{:S(2)}) collective-permute-start(bf16[128,512]{1,0:T(8,128)(2,1)} %refs_11_.1), channel_id=1, source_target_pairs={{0,4},{1,5},{2,6},{3,7},{4,0},{5,1},{6,2},{7,3},{8,12},{9,13},{10,... | collective-permute-start | bytes 393224 | tf_op jit(solution)/shard_map/ppermute | solution.py:150
  12.0 14.1 %collective-permute-start.8 = (bf16[128,512]{1,0:T(8,128)(2,1)}, bf16[128,512]{1,0:T(8,128)(2,1)S(1)}, u32[]{:S(2)}, u32[]{:S(2)}) collective-permute-start(bf16[128,512]{1,0:T(8,128)(2,1)} %refs_11_.1), channel_id=1, source_target_pairs={{0,2},{1,3},{2,0},{3,1},{4,6},{5,7},{6,4},{7,5},{8,10},{9,11},{10,... | collective-permute-start | bytes 393224 | tf_op jit(solution)/shard_map/ppermute | solution.py:150
  12.4 13.7 %collective-permute-start.7 = (bf16[128,512]{1,0:T(8,128)(2,1)}, bf16[128,512]{1,0:T(8,128)(2,1)S(1)}, u32[]{:S(2)}, u32[]{:S(2)}) collective-permute-start(bf16[128,512]{1,0:T(8,128)(2,1)} %refs_11_.1), channel_id=1, source_target_pairs={{0,1},{1,0},{2,3},{3,2},{4,5},{5,4},{6,7},{7,6},{8,9},{9,8},{10,11... | collective-permute-start | bytes 393224 | tf_op jit(solution)/shard_map/ppermute | solution.py:150
  12.4 14.2 %collective-permute-start.12 = (bf16[128,512]{1,0:T(8,128)(2,1)}, bf16[128,512]{1,0:T(8,128)(2,1)S(1)}, u32[]{:S(2)}, u32[]{:S(2)}) collective-permute-start(bf16[128,512]{1,0:T(8,128)(2,1)} %refs_11_.1), channel_id=1, source_target_pairs={{0,6},{1,7},{2,4},{3,5},{4,2},{5,3},{6,0},{7,1},{8,14},{9,15},{10,... | collective-permute-start | bytes 393224 | tf_op jit(solution)/shard_map/ppermute | solution.py:150
  15.4 11.2 %collective-permute-start.4 = (bf16[128,512]{1,0:T(8,128)(2,1)S(1)}, bf16[128,512]{1,0:T(8,128)(2,1)S(1)}, u32[]{:S(2)}, u32[]{:S(2)}) collective-permute-start(bf16[128,512]{1,0:T(8,128)(2,1)S(1)} %collective-permute-done.3.refs_7_), channel_id=1, source_target_pairs={{0,1},{1,0},{2,3},{3,2},{4,5},{5,4},{6,7},{7,6},{8,9},{9,8},{10,11... | collective-permute-start | bytes 393224 | tf_op jit(solution)/shard_map/ppermute | solution.py:150
  16.9 14.1 %all-to-all-start = ((s32[8,1,128]{2,1,0:T(1,128)}), s32[8,1,128]{2,1,0:T(1,128)S(1)}, u32[]{:S(2)}, u32[]{:S(2)}) async-start(s32[8,1,128]{2,1,0:T(1,128)} %broadcast_in_dim.2), calls=%async_computation | async-start | bytes 8192 | tf_op jit(solution)/shard_map/all_to_all | solution.py:158
  25.5 6.0 %collective-permute-start.2 = (bf16[128,512]{1,0:T(8,128)(2,1)S(1)}, bf16[128,512]{1,0:T(8,128)(2,1)S(1)}, u32[]{:S(2)}, u32[]{:S(2)}) collective-permute-start(bf16[128,512]{1,0:T(8,128)(2,1)S(1)} %collective-permute-done.1.refs_5_), channel_id=1, source_target_pairs={{0,1},{1,0},{2,3},{3,2},{4,5},{5,4},{6,7},{7,6},{8,9},{9,8},{10,11... | collective-permute-start | bytes 393224 | tf_op jit(solution)/shard_map/ppermute | solution.py:150
  26.0 5.5 %collective-permute-start.6 = (bf16[128,512]{1,0:T(8,128)(2,1)S(1)}, bf16[128,512]{1,0:T(8,128)(2,1)S(1)}, u32[]{:S(2)}, u32[]{:S(2)}) collective-permute-start(bf16[128,512]{1,0:T(8,128)(2,1)S(1)} %collective-permute-done.5.refs_9_), channel_id=1, source_target_pairs={{0,1},{1,0},{2,3},{3,2},{4,5},{5,4},{6,7},{7,6},{8,9},{9,8},{10,11... | collective-permute-start | bytes 393224 | tf_op jit(solution)/shard_map/ppermute | solution.py:150
  26.1 5.5 %collective-permute-start.11 = (bf16[128,512]{1,0:T(8,128)(2,1)S(1)}, bf16[128,512]{1,0:T(8,128)(2,1)S(1)}, u32[]{:S(2)}, u32[]{:S(2)}) collective-permute-start(bf16[128,512]{1,0:T(8,128)(2,1)S(1)} %collective-permute-done.10.refs_15_), channel_id=1, source_target_pairs={{0,1},{1,0},{2,3},{3,2},{4,5},{5,4},{6,7},{7,6},{8,9},{9,8},{10,11... | collective-permute-start | bytes 393224 | tf_op jit(solution)/shard_map/ppermute | solution.py:150
  26.5 5.0 %collective-permute-start.9 = (bf16[128,512]{1,0:T(8,128)(2,1)S(1)}, bf16[128,512]{1,0:T(8,128)(2,1)S(1)}, u32[]{:S(2)}, u32[]{:S(2)}) collective-permute-start(bf16[128,512]{1,0:T(8,128)(2,1)S(1)} %collective-permute-done.8.refs_13_), channel_id=1, source_target_pairs={{0,1},{1,0},{2,3},{3,2},{4,5},{5,4},{6,7},{7,6},{8,9},{9,8},{10,11... | collective-permute-start | bytes 393224 | tf_op jit(solution)/shard_map/ppermute | solution.py:150
  26.6 5.0 %collective-permute-start.13 = (bf16[128,512]{1,0:T(8,128)(2,1)S(1)}, bf16[128,512]{1,0:T(8,128)(2,1)S(1)}, u32[]{:S(2)}, u32[]{:S(2)}) collective-permute-start(bf16[128,512]{1,0:T(8,128)(2,1)S(1)} %collective-permute-done.12.refs_17_), channel_id=1, source_target_pairs={{0,1},{1,0},{2,3},{3,2},{4,5},{5,4},{6,7},{7,6},{8,9},{9,8},{10,11... | collective-permute-start | bytes 393224 | tf_op jit(solution)/shard_map/ppermute | solution.py:150
  31.0 0.7 %copy-start.3 = (s32[8]{0:T(128)S(1)}, s32[8]{0:T(128)}, u32[]{:S(2)}) copy-start(s32[8]{0:T(128)} %refs_0_.1) | copy-start | bytes 100
  31.7 1.0 %copy-start = (bf16[128,2048]{1,0:T(8,128)(2,1)S(1)}, bf16[128,2048]{1,0:T(8,128)(2,1)}, u32[]{:S(2)}) copy-start(bf16[128,2048]{1,0:T(8,128)(2,1)} %refs_2_.1) | copy-start | bytes 1572868
  32.7 0.9 %copy-start.1 = (bf16[128,512]{1,0:T(8,128)(2,1)S(1)}, bf16[128,512]{1,0:T(8,128)(2,1)}, u32[]{:S(2)}) copy-start(bf16[128,512]{1,0:T(8,128)(2,1)} %refs_3_.1) | copy-start | bytes 393220
  33.6 0.9 %copy-start.2 = (bf16[128,512]{1,0:T(8,128)(2,1)S(1)}, bf16[128,512]{1,0:T(8,128)(2,1)}, u32[]{:S(2)}) copy-start(bf16[128,512]{1,0:T(8,128)(2,1)} %refs_11_.1) | copy-start | bytes 393220

commit v2 on v0

--- a/solution.py
+++ b/solution.py
@@ -1,14 +1,19 @@
 import jax
 import jax.numpy as jnp
 from jax import lax
+from jax.experimental import pallas as pl
+from jax.experimental.pallas import tpu as pltpu
 from jax.sharding import PartitionSpec as P
 
 KEY_VALUE_HEADS = 4
 HEAD_WIDTH = 128
 REACH = 2
+GATHER_SHARDS = 8
+POS_ROWS = 8
 
 
 masked_value = -1e30
+EXP2_SCALE = 1.4426950408889634 / HEAD_WIDTH**0.5
 
 
 def shifted(block, axis, distance):
@@ -54,7 +59,7 @@
     return jnp.concatenate(results, axis=1).astype(jnp.bfloat16)
 
 
-def on_device(queries, keys, values, doc_lengths, loader_pos):
+def routed(queries, keys, values, doc_lengths, loader_pos):
     routed_rows = queries.shape[0]
     shards = lax.axis_size("ctx")
     cap_rows = routed_rows // shards
@@ -96,6 +101,186 @@
     return returned[jnp.argsort(order)]
 
 
+def lanes(head):
+    return slice(head * HEAD_WIDTH, (head + 1) * HEAD_WIDTH)
+
+
+def after(x, *earlier):
+    return lax.optimization_barrier((x, *earlier))[0]
+
+
+def pack_kernel(k_ref, v_ref, pos_ref, out_ref, pos_vmem, sems):
+    rows = k_ref.shape[0]
+    copies = [pltpu.make_async_copy(pos_ref, pos_vmem, sems.at[2 * KEY_VALUE_HEADS])]
+    for i, ref in enumerate((k_ref, v_ref)):
+        for head in range(KEY_VALUE_HEADS):
+            slab = i * KEY_VALUE_HEADS + head
+            copies.append(
+                pltpu.make_async_copy(
+                    ref.at[:, lanes(head)], out_ref.at[slab * rows : (slab + 1) * rows, :], sems.at[slab]
+                )
+            )
+    for copy in copies:
+        copy.start()
+    copies[0].wait()
+    pos = pos_vmem[...]
+    row = lax.broadcasted_iota(jnp.int32, (POS_ROWS, rows), 0)
+    digits = jnp.where(row == 0, pos % 128, pos // 128)
+    out_ref[2 * KEY_VALUE_HEADS * rows :, :] = digits.astype(jnp.float32).astype(jnp.bfloat16)
+    for copy in copies[1:]:
+        copy.wait()
+
+
+def positions(block_ref):
+    at = block_ref.shape[0] - POS_ROWS
+    both = block_ref[at:, :].astype(jnp.float32)
+    return both[0:1] + 128.0 * both[1:2]
+
+
+def keys_of(block_refs, rows, head):
+    return jnp.concatenate([r[head * rows : (head + 1) * rows, :] for r in block_refs], axis=0)
+
+
+def values_of(block_refs, rows, head):
+    return keys_of(block_refs, rows, KEY_VALUE_HEADS + head)
+
+
+def write_bias(bias_ref, block_refs, q_pos, q_first):
+    rows = bias_ref.shape[0]
+    for s, ref in enumerate(block_refs):
+        k_pos = positions(ref)
+        allowed = (k_pos <= q_pos) & (k_pos >= q_first)
+        bias_ref[:, s * rows : (s + 1) * rows] = jnp.where(allowed, 0.0, masked_value)
+
+
+def stacked(ref, head, group):
+    return jnp.concatenate([ref[:, lanes(head * group + g)] for g in range(group)], axis=0)
+
+
+def fold_kernel(shards, first, last, *refs):
+    if first:
+        (doc_ref, q_ref), refs = refs[:2], refs[2:]
+    else:
+        (q_ref, where_ref, mean_ref, level_ref), refs = refs[:4], refs[4:]
+    block_refs, refs = refs[:shards], refs[shards:]
+    outs, (bias_ref, weight_ref) = refs[:-2], refs[-2:]
+    rows = q_ref.shape[0]
+    group = q_ref.shape[1] // HEAD_WIDTH // KEY_VALUE_HEADS
+    if first:
+        square = (rows, rows)
+        diagonal = lax.broadcasted_iota(jnp.int32, square, 0) == lax.broadcasted_iota(jnp.int32, square, 1)
+        q_pos = jnp.sum(jnp.where(diagonal, positions(block_refs[0]), 0.0), axis=1, keepdims=True)
+        end, q_first = jnp.int32(0), jnp.zeros_like(q_pos)
+        for j in range(doc_ref.shape[0]):
+            end = end + doc_ref[j]
+            limit = end.astype(jnp.float32)
+            q_first = jnp.where(q_pos >= limit, limit, q_first)
+        outs[0][0] = jnp.broadcast_to(q_pos, (rows, HEAD_WIDTH))
+        outs[0][1] = jnp.broadcast_to(q_first, (rows, HEAD_WIDTH))
+        outs = outs[1:]
+    else:
+        q_pos, q_first = where_ref[0], where_ref[1]
+    write_bias(bias_ref, block_refs, q_pos, q_first)
+
+    for head in range(KEY_VALUE_HEADS):
+        k_part, v_part = keys_of(block_refs, rows, head), values_of(block_refs, rows, head)
+        raw = lax.dot_general(
+            stacked(q_ref, head, group),
+            k_part,
+            (((1,), (1,)), ((), ())),
+            preferred_element_type=jnp.float32,
+        )
+        tops, totals, before = [], [], []
+        for g in range(group):
+            part = slice(g * rows, (g + 1) * rows)
+            scores = raw[part] + bias_ref[...]
+            top = jnp.max(scores, axis=1, keepdims=True)
+            if first:
+                weight = jnp.exp2((scores - top) * EXP2_SCALE)
+                total = jnp.sum(weight, axis=1, keepdims=True)
+            else:
+                level = level_ref[head * group + g]
+                top = jnp.maximum(top, level)
+                weight = jnp.exp2((scores - jnp.tile(top, (1, shards))) * EXP2_SCALE)
+                before.append(jnp.exp2((level - top) * EXP2_SCALE))
+                total = before[-1] + jnp.sum(weight, axis=1, keepdims=True)
+            weight_ref[part] = weight.astype(jnp.bfloat16)
+            tops.append(top)
+            totals.append(total)
+        mixed = jnp.dot(weight_ref[...], v_part, preferred_element_type=jnp.float32)
+        for g in range(group):
+            q_head = head * group + g
+            mean = mixed[g * rows : (g + 1) * rows]
+            if not first:
+                mean = mean + before[g] * mean_ref[q_head]
+            mean = mean / totals[g]
+            if last:
+                outs[0][:, lanes(q_head)] = mean.astype(jnp.bfloat16)
+            else:
+                outs[0][q_head] = mean
+                level = tops[g] + jnp.log2(totals[g]) * (1.0 / EXP2_SCALE)
+                outs[1][q_head] = jnp.broadcast_to(level, (rows, HEAD_WIDTH))
+
+
+def gathered(queries, keys, values, doc_lengths, loader_pos):
+    shards = lax.axis_size("ctx")
+    rows = queries.shape[0]
+    heads = queries.shape[1] // HEAD_WIDTH
+    vmem, smem = pl.BlockSpec(memory_space=pltpu.VMEM), pl.BlockSpec(memory_space=pltpu.SMEM)
+    hbm = pl.BlockSpec(memory_space=pl.ANY)
+    per_head = jax.ShapeDtypeStruct((heads, rows, HEAD_WIDTH), jnp.float32)
+
+    def swap(x, distance):
+        return lax.ppermute(x, "ctx", [(i, i ^ distance) for i in range(shards)])
+
+    def fold(name, blocks, *state, last=False):
+        n, first = len(blocks), not state
+        out_shape = (per_head, per_head)
+        if first:
+            out_shape = (jax.ShapeDtypeStruct((2, rows, HEAD_WIDTH), jnp.float32), *out_shape)
+        if last:
+            out_shape = (jax.ShapeDtypeStruct(queries.shape, queries.dtype),)
+        return pl.pallas_call(
+            lambda *refs: fold_kernel(n, first, last, *refs),
+            out_shape=out_shape,
+            in_specs=([smem] if first else []) + [vmem] * (1 + len(state) + n),
+            out_specs=(vmem,) * len(out_shape),
+            scratch_shapes=[
+                pltpu.VMEM((rows, n * rows), jnp.float32),
+                pltpu.VMEM((heads // KEY_VALUE_HEADS * rows, n * rows), jnp.bfloat16),
+            ],
+            compiler_params=pltpu.CompilerParams(vmem_limit_bytes=32 << 20),
+            name=name,
+        )(*([doc_lengths] if first else []), queries, *state, *blocks)
+
+    slabs = 2 * KEY_VALUE_HEADS
+    own = pl.pallas_call(
+        pack_kernel,
+        out_shape=jax.ShapeDtypeStruct((slabs * rows + POS_ROWS, HEAD_WIDTH), keys.dtype),
+        in_specs=[hbm, hbm, hbm],
+        out_specs=vmem,
+        scratch_shapes=[
+            pltpu.VMEM((1, rows), jnp.int32),
+            pltpu.SemaphoreType.DMA((slabs + 1,)),
+        ],
+        name="pack",
+    )(keys, values, loader_pos.reshape(1, rows))
+    six = swap(own, 6)
+    two = swap(own, 2)
+    four = swap(six, 2)
+    where, *state = fold("early", [own, six, two, swap(after(own, six), 1), swap(six, 1)])
+    four = after(four, *state)
+    state = fold("middle", [swap(two, 1), four], where, *state)
+    return fold("last", [swap(four, 1)], where, *state, last=True)[0]
+
+
+def on_device(queries, keys, values, doc_lengths, loader_pos):
+    shards = lax.axis_size("ctx")
+    if shards == GATHER_SHARDS:
+        return gathered(queries, keys, values, doc_lengths, loader_pos)
+    return routed(queries, keys, values, doc_lengths, loader_pos)
+
+
 def solution(mesh):
     placed = (
         P(("grp", "ctx"), None),

time: 94.9 us -> 29.4 us (0.31)
  starting transfers between devices: 39.7 us -> 10.1 us
  local copies, waits for them, and re-layouts: 17.7 us -> 0.95 us
  waiting for transfers between devices: 22.2 us -> 9.92 us
  other arithmetic: 10.2 us -> 0 us
  Pallas kernels: 0 us -> 8.21 us
  matrix products: 3.95 us -> 0 us
    all_to_all x5 -> x0, starting transfers between devices: 27.3 us -> none  [the longest x1 10.1 us: on_device(): lax.all_to_all(outgoing, 'ctx', split_axis=0, concat_axis=0, tiled=True)]
    all_to_all x5 -> x0, waiting for transfers between devices: 21.3 us -> none  [the longest x1 12.1 us: on_device(): lax.all_to_all(outgoing, 'ctx', split_axis=0, concat_axis=0, tiled=True)]
    gather x11 -> x0, local copies, waits for them, and re-layouts: 12.4 us -> none  [the longest x1 1.73 us: on_device(): outgoing = packed_out[local].reshape(shards, cap_rows, -1)]
    ppermute x4 -> x7, waiting for transfers between devices: 0.88 us -> 9.92 us  [swap(): return lax.ppermute(x, 'ctx', [(i, i ^ distance) for i in range(shards)])]
    pallas_call x0 -> x4, Pallas kernels: none -> 8.21 us  [the longest x3 6.48 us: fold(): pl.pallas_call(lambda *refs: fold_kernel(n, first, last, *refs), out_shap...]
    sort x3 -> x0, other arithmetic: 7.68 us -> none  [the longest x1 2.61 us: on_device(): return returned[jnp.argsort(order)]]
    dot_general x8 -> x0, matrix products: 3.95 us -> none  [the longest x4 2.82 us: attend(): jnp.einsum('tgd,wd->gtw', query_head_rows[:, head_number], k_part, prefer...]
    unnamed x20 -> x6, local copies, waits for them, and re-layouts: 3.49 us -> 0.95 us
  transfers between devices with their start and end apart: 9 -> 7, of which waited for: 5 -> 3; matrix products, arithmetic and copies ran while one was open for 15% -> 0% of each run, Pallas kernels for 0% -> 16%
where the time goes in v2:
time: 29.4 us; the launch traced here: 29.2 us
  starting transfers between devices  10.1 us (34%)
  waiting for transfers between devices  9.92 us (34%)
  Pallas kernels  8.21 us (28%)
  local copies, waits for them, and re-layouts  0.95 us (3%)
    ppermute x7, starting transfers between devices, swap(): return lax.ppermute(x, 'ctx', [(i, i ^ distance) for i in range(shards)])  10.1 us
    ppermute x7, waiting for transfers between devices, swap(): return lax.ppermute(x, 'ctx', [(i, i ^ distance) for i in range(shards)])  9.92 us
    pallas_call x3, Pallas kernels, fold(): pl.pallas_call(lambda *refs: fold_kernel(n, first, last, *refs), out_shap...  6.48 us
    pallas_call x1, Pallas kernels, gathered(): pl.pallas_call(pack_kernel, out_shape=jax.ShapeDtypeStruct((slabs * rows...  1.73 us
    unnamed x6, local copies, waits for them, and re-layouts  0.95 us
  transfers between devices with their start and end apart: 7, of which 3 were waited for; matrix products, arithmetic and copies ran while one was open for 0% of the time, Pallas kernels for 16%

profile of v2, /device:TPU:0, one launch (start us, length us, event | category | flops | bytes accessed | tf_op | source)
XLA Modules:
  0.0 29.2 jit_solution(10628598214090400038)
XLA Ops:
  0.0 0.0 copy-start
  0.0 0.0 copy-start.2
  0.0 1.7 %pack.1.refs_2_ = bf16[1032,128]{1,0:T(8,128)(2,1)} custom-call(bf16[128,512]{1,0:T(8,128)(2,1)} %k_ref.1, bf16[128,512]{1,0:T(8,128)(2,1)} %v_ref.1, s32[1,128]{1,0:T(1,128)} %bitcast.1), custom_call_target="tpu_custom_call" | custom-call | tf_op jit(solution)/shard_map/pack/pallas_call | solution.py:257
  1.7 5.1 %collective-permute-start = (bf16[1032,128]{1,0:T(8,128)(2,1)}, bf16[1032,128]{1,0:T(8,128)(2,1)S(1)}, u32[]{:S(2)}, u32[]{:S(2)}) collective-permute-start(bf16[1032,128]{1,0:T(8,128)(2,1)} %pack.1.refs_2_), channel_id=1, source_target_pairs={{0,6},{1,7},{2,4},{3,5},{4,2},{5,3},{6,0},{7,1},{8,14},{9,15},{10,... | collective-permute-start | bytes 792584 | tf_op jit(solution)/shard_map/ppermute | solution.py:234
  6.9 0.0 collective-permute-start.1
  6.9 7.5 %collective-permute-done.refs_3_ = bf16[1032,128]{1,0:T(8,128)(2,1)S(1)} collective-permute-done((bf16[1032,128]{1,0:T(8,128)(2,1)}, bf16[1032,128]{1,0:T(8,128)(2,1)S(1)}, u32[]{:S(2)}, u32[]{:S(2)}) %collective-permute-start) | collective-permute-done | bytes 264224 | tf_op jit(solution)/shard_map/ppermute | solution.py:234
  14.3 0.0 collective-permute-start.2
  14.3 0.5 %collective-permute-start.3 = (bf16[1032,128]{1,0:T(8,128)(2,1)S(1)}, bf16[1032,128]{1,0:T(8,128)(2,1)S(1)}, u32[]{:S(2)}, u32[]{:S(2)}) collective-permute-start(bf16[1032,128]{1,0:T(8,128)(2,1)S(1)} %collective-permute-done.refs_3_), channel_id=1, source_target_pairs={{0,1},{1,0},{2,3},{3,2},{4,5},{5,4},{6,7},{7,6},{8,9},{9,8},{10,11... | collective-permute-start | bytes 792584 | tf_op jit(solution)/shard_map/ppermute | solution.py:234
  14.8 4.5 %collective-permute-start.5 = (bf16[1032,128]{1,0:T(8,128)(2,1)S(1)}, bf16[1032,128]{1,0:T(8,128)(2,1)S(1)}, u32[]{:S(2)}, u32[]{:S(2)}) collective-permute-start(bf16[1032,128]{1,0:T(8,128)(2,1)S(1)} %collective-permute-done.refs_3_), channel_id=1, source_target_pairs={{0,2},{1,3},{2,0},{3,1},{4,6},{5,7},{6,4},{7,5},{8,10},{9,11},{10,... | collective-permute-start | bytes 792584 | tf_op jit(solution)/shard_map/ppermute | solution.py:234
  19.3 0.0 collective-permute-done.1.refs_4_
  19.3 0.0 collective-permute-start.4
  19.3 0.0 collective-permute-done.2.refs_5_
  19.3 0.0 collective-permute-done.3.refs_6_
  19.3 0.0 copy-done
  19.3 0.0 copy-done.2
  19.3 0.0 copy-start.1
  19.4 0.9 %copy-done.1 = bf16[1032,128]{1,0:T(8,128)(2,1)S(1)} copy-done((bf16[1032,128]{1,0:T(8,128)(2,1)S(1)}, bf16[1032,128]{1,0:T(8,128)(2,1)}, u32[]{:S(2)}) %copy-start.1) | copy-done | bytes 264216
  20.3 3.4 %early.1 = (f32[2,128,128]{2,1,0:T(8,128)S(1)}, f32[16,128,128]{2,1,0:T(8,128)S(1)}, f32[16,128,128]{2,1,0:T(8,128)S(1)}) custom-call(s32[8]{0:T(128)S(1)} %copy-done.2, bf16[128,2048]{1,0:T(8,128)(2,1)S(1)} %copy-done, bf16[1032,128]{1,0:T(8,128)(2,1)S(1)} %copy-done.1, bf16[1032,128]{1,0:T(8,128)(2,1)S(1)} %collective-permute-done.refs_3_, ...), custom_call_target="tpu_custom_call" | custom-call | tf_op jit(solution)/shard_map/early/pallas_call | solution.py:243
  23.7 2.1 %collective-permute-done.5.refs_5_ = bf16[1032,128]{1,0:T(8,128)(2,1)S(1)} collective-permute-done((bf16[1032,128]{1,0:T(8,128)(2,1)S(1)}, bf16[1032,128]{1,0:T(8,128)(2,1)S(1)}, u32[]{:S(2)}, u32[]{:S(2)}) %collective-permute-start.5) | collective-permute-done | bytes 264224 | tf_op jit(solution)/shard_map/ppermute | solution.py:234
  25.8 0.0 collective-permute-start.6
  25.8 0.0 collective-permute-done.4.refs_4_
  25.8 1.2 %middle.1 = (f32[16,128,128]{2,1,0:T(8,128)S(1)}, f32[16,128,128]{2,1,0:T(8,128)S(1)}) custom-call(bf16[128,2048]{1,0:T(8,128)(2,1)S(1)} %copy-done, f32[2,128,128]{2,1,0:T(8,128)S(1)} %get-tuple-element.13.refs_1_, f32[16,128,128]{2,1,0:T(8,128)S(1)} %get-tuple-element.14.refs_2_, f32[16,128,128]{2,1,0:T(8,128)S(1)} %get-tuple-element.15.refs_3_, ...), custom_call_target="tpu_custom_call" | custom-call | tf_op jit(solution)/shard_map/middle/pallas_call | solution.py:243
  27.0 0.4 %collective-permute-done.6.refs_4_ = bf16[1032,128]{1,0:T(8,128)(2,1)S(1)} collective-permute-done((bf16[1032,128]{1,0:T(8,128)(2,1)S(1)}, bf16[1032,128]{1,0:T(8,128)(2,1)S(1)}, u32[]{:S(2)}, u32[]{:S(2)}) %collective-permute-start.6) | collective-permute-done | bytes 264224 | tf_op jit(solution)/shard_map/ppermute | solution.py:234
  27.4 1.9 %last.1 = bf16[128,2048]{1,0:T(8,128)(2,1)} custom-call(bf16[128,2048]{1,0:T(8,128)(2,1)S(1)} %copy-done, f32[2,128,128]{2,1,0:T(8,128)S(1)} %get-tuple-element.13.refs_1_, f32[16,128,128]{2,1,0:T(8,128)S(1)} %get-tuple-element.17.refs_2_, f32[16,128,128]{2,1,0:T(8,128)S(1)} %get-tuple-element.18.refs_3_, bf16[1032,128]{1,0:T(8,128)(2,1)S(1)} %collective-permute-done.6.refs_4_), custom_call_target="tpu_custom_call" | custom-call | tf_op jit(solution)/shard_map/last/pallas_call | solution.py:243
Async XLA Ops:
  0.0 19.3 %copy-start = (bf16[128,2048]{1,0:T(8,128)(2,1)S(1)}, bf16[128,2048]{1,0:T(8,128)(2,1)}, u32[]{:S(2)}) copy-start(bf16[128,2048]{1,0:T(8,128)(2,1)} %refs_0_.5) | copy-start | bytes 1572868
  0.0 19.3 %copy-start.2 = (s32[8]{0:T(128)S(1)}, s32[8]{0:T(128)}, u32[]{:S(2)}) copy-start(s32[8]{0:T(128)} %refs_0_.3) | copy-start | bytes 100
  1.7 12.6 %collective-permute-start = (bf16[1032,128]{1,0:T(8,128)(2,1)}, bf16[1032,128]{1,0:T(8,128)(2,1)S(1)}, u32[]{:S(2)}, u32[]{:S(2)}) collective-permute-start(bf16[1032,128]{1,0:T(8,128)(2,1)} %pack.1.refs_2_), channel_id=1, source_target_pairs={{0,6},{1,7},{2,4},{3,5},{4,2},{5,3},{6,0},{7,1},{8,14},{9,15},{10,... | collective-permute-start | bytes 792584 | tf_op jit(solution)/shard_map/ppermute | solution.py:234
  6.9 12.5 %collective-permute-start.1 = (bf16[1032,128]{1,0:T(8,128)(2,1)}, bf16[1032,128]{1,0:T(8,128)(2,1)S(1)}, u32[]{:S(2)}, u32[]{:S(2)}) collective-permute-start(bf16[1032,128]{1,0:T(8,128)(2,1)} %pack.1.refs_2_), channel_id=1, source_target_pairs={{0,2},{1,3},{2,0},{3,1},{4,6},{5,7},{6,4},{7,5},{8,10},{9,11},{10,... | collective-permute-start | bytes 792584 | tf_op jit(solution)/shard_map/ppermute | solution.py:234
  14.3 5.0 %collective-permute-start.2 = (bf16[1032,128]{1,0:T(8,128)(2,1)}, bf16[1032,128]{1,0:T(8,128)(2,1)S(1)}, u32[]{:S(2)}, u32[]{:S(2)}) collective-permute-start(bf16[1032,128]{1,0:T(8,128)(2,1)} %pack.1.refs_2_), channel_id=1, source_target_pairs={{0,1},{1,0},{2,3},{3,2},{4,5},{5,4},{6,7},{7,6},{8,9},{9,8},{10,11... | collective-permute-start | bytes 792584 | tf_op jit(solution)/shard_map/ppermute | solution.py:234
  14.3 5.0 %collective-permute-start.3 = (bf16[1032,128]{1,0:T(8,128)(2,1)S(1)}, bf16[1032,128]{1,0:T(8,128)(2,1)S(1)}, u32[]{:S(2)}, u32[]{:S(2)}) collective-permute-start(bf16[1032,128]{1,0:T(8,128)(2,1)S(1)} %collective-permute-done.refs_3_), channel_id=1, source_target_pairs={{0,1},{1,0},{2,3},{3,2},{4,5},{5,4},{6,7},{7,6},{8,9},{9,8},{10,11... | collective-permute-start | bytes 792584 | tf_op jit(solution)/shard_map/ppermute | solution.py:234
  14.8 11.0 %collective-permute-start.5 = (bf16[1032,128]{1,0:T(8,128)(2,1)S(1)}, bf16[1032,128]{1,0:T(8,128)(2,1)S(1)}, u32[]{:S(2)}, u32[]{:S(2)}) collective-permute-start(bf16[1032,128]{1,0:T(8,128)(2,1)S(1)} %collective-permute-done.refs_3_), channel_id=1, source_target_pairs={{0,2},{1,3},{2,0},{3,1},{4,6},{5,7},{6,4},{7,5},{8,10},{9,11},{10,... | collective-permute-start | bytes 792584 | tf_op jit(solution)/shard_map/ppermute | solution.py:234
  19.3 6.5 %collective-permute-start.4 = (bf16[1032,128]{1,0:T(8,128)(2,1)S(1)}, bf16[1032,128]{1,0:T(8,128)(2,1)S(1)}, u32[]{:S(2)}, u32[]{:S(2)}) collective-permute-start(bf16[1032,128]{1,0:T(8,128)(2,1)S(1)} %collective-permute-done.1.refs_4_), channel_id=1, source_target_pairs={{0,1},{1,0},{2,3},{3,2},{4,5},{5,4},{6,7},{7,6},{8,9},{9,8},{10,11... | collective-permute-start | bytes 792584 | tf_op jit(solution)/shard_map/ppermute | solution.py:234
  19.3 1.0 %copy-start.1 = (bf16[1032,128]{1,0:T(8,128)(2,1)S(1)}, bf16[1032,128]{1,0:T(8,128)(2,1)}, u32[]{:S(2)}) copy-start(bf16[1032,128]{1,0:T(8,128)(2,1)} %pack.1.refs_2_) | copy-start | bytes 792580
  25.8 1.5 %collective-permute-start.6 = (bf16[1032,128]{1,0:T(8,128)(2,1)S(1)}, bf16[1032,128]{1,0:T(8,128)(2,1)S(1)}, u32[]{:S(2)}, u32[]{:S(2)}) collective-permute-start(bf16[1032,128]{1,0:T(8,128)(2,1)S(1)} %collective-permute-done.5.refs_5_), channel_id=1, source_target_pairs={{0,1},{1,0},{2,3},{3,2},{4,5},{5,4},{6,7},{7,6},{8,9},{9,8},{10,11... | collective-permute-start | bytes 792584 | tf_op jit(solution)/shard_map/ppermute | solution.py:234

commit v3 on v2

--- a/solution.py
+++ b/solution.py
@@ -163,7 +163,11 @@
     else:
         (q_ref, where_ref, mean_ref, level_ref), refs = refs[:4], refs[4:]
     block_refs, refs = refs[:shards], refs[shards:]
-    outs, (bias_ref, weight_ref) = refs[:-2], refs[-2:]
+    if last:
+        out_hbm, bias_ref, weight_ref, out_ref, sems = refs
+        outs, stores = (out_ref,), []
+    else:
+        outs, (bias_ref, weight_ref) = refs[:-2], refs[-2:]
     rows = q_ref.shape[0]
     group = q_ref.shape[1] // HEAD_WIDTH // KEY_VALUE_HEADS
     if first:
@@ -213,13 +217,22 @@
             mean = mixed[g * rows : (g + 1) * rows]
             if not first:
                 mean = mean + before[g] * mean_ref[q_head]
-            mean = mean / totals[g]
+            mean = mean * (1.0 / totals[g])
             if last:
                 outs[0][:, lanes(q_head)] = mean.astype(jnp.bfloat16)
             else:
                 outs[0][q_head] = mean
                 level = tops[g] + jnp.log2(totals[g]) * (1.0 / EXP2_SCALE)
                 outs[1][q_head] = jnp.broadcast_to(level, (rows, HEAD_WIDTH))
+        if last:
+            done = slice(head * group * HEAD_WIDTH, (head + 1) * group * HEAD_WIDTH)
+            stores.append(
+                pltpu.make_async_copy(out_ref.at[:, done], out_hbm.at[:, done], sems.at[head])
+            )
+            stores[-1].start()
+    if last:
+        for store in stores:
+            store.wait()
 
 
 def gathered(queries, keys, values, doc_lengths, loader_pos):
@@ -244,10 +257,15 @@
             lambda *refs: fold_kernel(n, first, last, *refs),
             out_shape=out_shape,
             in_specs=([smem] if first else []) + [vmem] * (1 + len(state) + n),
-            out_specs=(vmem,) * len(out_shape),
+            out_specs=(hbm if last else vmem,) * len(out_shape),
             scratch_shapes=[
                 pltpu.VMEM((rows, n * rows), jnp.float32),
                 pltpu.VMEM((heads // KEY_VALUE_HEADS * rows, n * rows), jnp.bfloat16),
+            ]
+            + last
+            * [
+                pltpu.VMEM(queries.shape, queries.dtype),
+                pltpu.SemaphoreType.DMA((KEY_VALUE_HEADS,)),
             ],
             compiler_params=pltpu.CompilerParams(vmem_limit_bytes=32 << 20),
             name=name,
@@ -256,7 +274,7 @@
     slabs = 2 * KEY_VALUE_HEADS
     own = pl.pallas_call(
         pack_kernel,
-        out_shape=jax.ShapeDtypeStruct((slabs * rows + POS_ROWS, HEAD_WIDTH), keys.dtype),
+        out_shape=pltpu.VMEM((slabs * rows + POS_ROWS, HEAD_WIDTH), keys.dtype),
         in_specs=[hbm, hbm, hbm],
         out_specs=vmem,
         scratch_shapes=[

time: 29.4 us -> 28.4 us (0.966)
  local copies, waits for them, and re-layouts: 0.95 us -> 0.01 us
  Pallas kernels: 8.21 us -> 7.46 us
  waiting for transfers between devices: 9.92 us -> 10.6 us
    unnamed x6 -> x4, local copies, waits for them, and re-layouts: 0.95 us -> 0.01 us
    pallas_call x1, Pallas kernels: 1.73 us -> 1.03 us  [gathered(): pl.pallas_call(pack_kernel, out_shape=pltpu.VMEM((slabs * rows + POS_ROWS...]
    ppermute x7, waiting for transfers between devices: 9.92 us -> 10.6 us  [swap(): return lax.ppermute(x, 'ctx', [(i, i ^ distance) for i in range(shards)])]
  transfers between devices with their start and end apart: 7 -> 7, of which waited for: 3 -> 3; matrix products, arithmetic and copies ran while one was open for 0% -> 0% of each run, Pallas kernels for 16% -> 17%
where the time goes in v3:
time: 28.4 us; the launch traced here: 28.2 us
  waiting for transfers between devices  10.6 us (37%)
  starting transfers between devices  10.1 us (36%)
  Pallas kernels  7.46 us (26%)
    ppermute x7, waiting for transfers between devices, swap(): return lax.ppermute(x, 'ctx', [(i, i ^ distance) for i in range(shards)])  10.6 us
    ppermute x7, starting transfers between devices, swap(): return lax.ppermute(x, 'ctx', [(i, i ^ distance) for i in range(shards)])  10.1 us
    pallas_call x3, Pallas kernels, fold(): pl.pallas_call(lambda *refs: fold_kernel(n, first, last, *refs), out_shap...  6.44 us
    pallas_call x1, Pallas kernels, gathered(): pl.pallas_call(pack_kernel, out_shape=pltpu.VMEM((slabs * rows + POS_ROWS...  1.03 us
  transfers between devices with their start and end apart: 7, of which 3 were waited for; matrix products, arithmetic and copies ran while one was open for 0% of the time, Pallas kernels for 17%

profile of v3, /device:TPU:0, one launch (start us, length us, event | category | flops | bytes accessed | tf_op | source)
XLA Modules:
  0.0 28.2 jit_solution(4849875462441867144)
XLA Ops:
  0.0 0.0 copy-start
  0.0 0.0 copy-start.1
  0.0 1.0 %pack.1.refs_2_ = bf16[1032,128]{1,0:T(8,128)(2,1)S(1)} custom-call(bf16[128,512]{1,0:T(8,128)(2,1)} %k_ref.1, bf16[128,512]{1,0:T(8,128)(2,1)} %v_ref.1, s32[1,128]{1,0:T(1,128)} %bitcast.1), custom_call_target="tpu_custom_call" | custom-call | tf_op jit(solution)/shard_map/pack/pallas_call | solution.py:275
  1.0 5.1 %collective-permute-start = (bf16[1032,128]{1,0:T(8,128)(2,1)S(1)}, bf16[1032,128]{1,0:T(8,128)(2,1)S(1)}, u32[]{:S(2)}, u32[]{:S(2)}) collective-permute-start(bf16[1032,128]{1,0:T(8,128)(2,1)S(1)} %pack.1.refs_2_), channel_id=1, source_target_pairs={{0,6},{1,7},{2,4},{3,5},{4,2},{5,3},{6,0},{7,1},{8,14},{9,15},{10,... | collective-permute-start | bytes 792584 | tf_op jit(solution)/shard_map/ppermute | solution.py:247
  6.2 0.0 collective-permute-start.1
  6.2 7.3 %collective-permute-done.refs_3_ = bf16[1032,128]{1,0:T(8,128)(2,1)S(1)} collective-permute-done((bf16[1032,128]{1,0:T(8,128)(2,1)S(1)}, bf16[1032,128]{1,0:T(8,128)(2,1)S(1)}, u32[]{:S(2)}, u32[]{:S(2)}) %collective-permute-start) | collective-permute-done | bytes 264224 | tf_op jit(solution)/shard_map/ppermute | solution.py:247
  13.4 0.0 collective-permute-start.2
  13.4 0.5 %collective-permute-start.3 = (bf16[1032,128]{1,0:T(8,128)(2,1)S(1)}, bf16[1032,128]{1,0:T(8,128)(2,1)S(1)}, u32[]{:S(2)}, u32[]{:S(2)}) collective-permute-start(bf16[1032,128]{1,0:T(8,128)(2,1)S(1)} %collective-permute-done.refs_3_), channel_id=1, source_target_pairs={{0,1},{1,0},{2,3},{3,2},{4,5},{5,4},{6,7},{7,6},{8,9},{9,8},{10,11... | collective-permute-start | bytes 792584 | tf_op jit(solution)/shard_map/ppermute | solution.py:247
  13.9 4.5 %collective-permute-start.5 = (bf16[1032,128]{1,0:T(8,128)(2,1)S(1)}, bf16[1032,128]{1,0:T(8,128)(2,1)S(1)}, u32[]{:S(2)}, u32[]{:S(2)}) collective-permute-start(bf16[1032,128]{1,0:T(8,128)(2,1)S(1)} %collective-permute-done.refs_3_), channel_id=1, source_target_pairs={{0,2},{1,3},{2,0},{3,1},{4,6},{5,7},{6,4},{7,5},{8,10},{9,11},{10,... | collective-permute-start | bytes 792584 | tf_op jit(solution)/shard_map/ppermute | solution.py:247
  18.4 0.0 collective-permute-done.1.refs_4_
  18.4 0.0 collective-permute-start.4
  18.4 0.0 collective-permute-done.2.refs_5_
  18.4 0.0 collective-permute-done.3.refs_6_
  18.4 0.0 copy-done
  18.4 0.0 copy-done.1
  18.4 3.4 %early.1 = (f32[2,128,128]{2,1,0:T(8,128)S(1)}, f32[16,128,128]{2,1,0:T(8,128)S(1)}, f32[16,128,128]{2,1,0:T(8,128)S(1)}) custom-call(s32[8]{0:T(128)S(1)} %copy-done.1, bf16[128,2048]{1,0:T(8,128)(2,1)S(1)} %copy-done, bf16[1032,128]{1,0:T(8,128)(2,1)S(1)} %pack.1.refs_2_, bf16[1032,128]{1,0:T(8,128)(2,1)S(1)} %collective-permute-done.refs_3_, ...), custom_call_target="tpu_custom_call" | custom-call | tf_op jit(solution)/shard_map/early/pallas_call | solution.py:256
  21.9 3.1 %collective-permute-done.5.refs_5_ = bf16[1032,128]{1,0:T(8,128)(2,1)S(1)} collective-permute-done((bf16[1032,128]{1,0:T(8,128)(2,1)S(1)}, bf16[1032,128]{1,0:T(8,128)(2,1)S(1)}, u32[]{:S(2)}, u32[]{:S(2)}) %collective-permute-start.5) | collective-permute-done | bytes 264224 | tf_op jit(solution)/shard_map/ppermute | solution.py:247
  24.9 0.0 collective-permute-start.6
  24.9 0.0 collective-permute-done.4.refs_4_
  24.9 1.3 %middle.1 = (f32[16,128,128]{2,1,0:T(8,128)S(1)}, f32[16,128,128]{2,1,0:T(8,128)S(1)}) custom-call(bf16[128,2048]{1,0:T(8,128)(2,1)S(1)} %copy-done, f32[2,128,128]{2,1,0:T(8,128)S(1)} %get-tuple-element.13.refs_1_, f32[16,128,128]{2,1,0:T(8,128)S(1)} %get-tuple-element.14.refs_2_, f32[16,128,128]{2,1,0:T(8,128)S(1)} %get-tuple-element.15.refs_3_, ...), custom_call_target="tpu_custom_call" | custom-call | tf_op jit(solution)/shard_map/middle/pallas_call | solution.py:256
  26.2 0.3 collective-permute-done.6.refs_4_
  26.4 1.8 %last.1 = bf16[128,2048]{1,0:T(8,128)(2,1)} custom-call(bf16[128,2048]{1,0:T(8,128)(2,1)S(1)} %copy-done, f32[2,128,128]{2,1,0:T(8,128)S(1)} %get-tuple-element.13.refs_1_, f32[16,128,128]{2,1,0:T(8,128)S(1)} %get-tuple-element.17.refs_2_, f32[16,128,128]{2,1,0:T(8,128)S(1)} %get-tuple-element.18.refs_3_, bf16[1032,128]{1,0:T(8,128)(2,1)S(1)} %collective-permute-done.6.refs_4_), custom_call_target="tpu_custom_call" | custom-call | tf_op jit(solution)/shard_map/last/pallas_call | solution.py:256
Async XLA Ops:
  0.0 18.4 %copy-start = (bf16[128,2048]{1,0:T(8,128)(2,1)S(1)}, bf16[128,2048]{1,0:T(8,128)(2,1)}, u32[]{:S(2)}) copy-start(bf16[128,2048]{1,0:T(8,128)(2,1)} %refs_0_.5) | copy-start | bytes 1572868
  0.0 18.4 %copy-start.1 = (s32[8]{0:T(128)S(1)}, s32[8]{0:T(128)}, u32[]{:S(2)}) copy-start(s32[8]{0:T(128)} %refs_0_.3) | copy-start | bytes 100
  1.0 12.4 %collective-permute-start = (bf16[1032,128]{1,0:T(8,128)(2,1)S(1)}, bf16[1032,128]{1,0:T(8,128)(2,1)S(1)}, u32[]{:S(2)}, u32[]{:S(2)}) collective-permute-start(bf16[1032,128]{1,0:T(8,128)(2,1)S(1)} %pack.1.refs_2_), channel_id=1, source_target_pairs={{0,6},{1,7},{2,4},{3,5},{4,2},{5,3},{6,0},{7,1},{8,14},{9,15},{10,... | collective-permute-start | bytes 792584 | tf_op jit(solution)/shard_map/ppermute | solution.py:247
  6.2 12.2 %collective-permute-start.1 = (bf16[1032,128]{1,0:T(8,128)(2,1)S(1)}, bf16[1032,128]{1,0:T(8,128)(2,1)S(1)}, u32[]{:S(2)}, u32[]{:S(2)}) collective-permute-start(bf16[1032,128]{1,0:T(8,128)(2,1)S(1)} %pack.1.refs_2_), channel_id=1, source_target_pairs={{0,2},{1,3},{2,0},{3,1},{4,6},{5,7},{6,4},{7,5},{8,10},{9,11},{10,... | collective-permute-start | bytes 792584 | tf_op jit(solution)/shard_map/ppermute | solution.py:247
  13.4 5.0 %collective-permute-start.2 = (bf16[1032,128]{1,0:T(8,128)(2,1)S(1)}, bf16[1032,128]{1,0:T(8,128)(2,1)S(1)}, u32[]{:S(2)}, u32[]{:S(2)}) collective-permute-start(bf16[1032,128]{1,0:T(8,128)(2,1)S(1)} %pack.1.refs_2_), channel_id=1, source_target_pairs={{0,1},{1,0},{2,3},{3,2},{4,5},{5,4},{6,7},{7,6},{8,9},{9,8},{10,11... | collective-permute-start | bytes 792584 | tf_op jit(solution)/shard_map/ppermute | solution.py:247
  13.4 5.0 %collective-permute-start.3 = (bf16[1032,128]{1,0:T(8,128)(2,1)S(1)}, bf16[1032,128]{1,0:T(8,128)(2,1)S(1)}, u32[]{:S(2)}, u32[]{:S(2)}) collective-permute-start(bf16[1032,128]{1,0:T(8,128)(2,1)S(1)} %collective-permute-done.refs_3_), channel_id=1, source_target_pairs={{0,1},{1,0},{2,3},{3,2},{4,5},{5,4},{6,7},{7,6},{8,9},{9,8},{10,11... | collective-permute-start | bytes 792584 | tf_op jit(solution)/shard_map/ppermute | solution.py:247
  13.9 11.0 %collective-permute-start.5 = (bf16[1032,128]{1,0:T(8,128)(2,1)S(1)}, bf16[1032,128]{1,0:T(8,128)(2,1)S(1)}, u32[]{:S(2)}, u32[]{:S(2)}) collective-permute-start(bf16[1032,128]{1,0:T(8,128)(2,1)S(1)} %collective-permute-done.refs_3_), channel_id=1, source_target_pairs={{0,2},{1,3},{2,0},{3,1},{4,6},{5,7},{6,4},{7,5},{8,10},{9,11},{10,... | collective-permute-start | bytes 792584 | tf_op jit(solution)/shard_map/ppermute | solution.py:247
  18.4 6.5 %collective-permute-start.4 = (bf16[1032,128]{1,0:T(8,128)(2,1)S(1)}, bf16[1032,128]{1,0:T(8,128)(2,1)S(1)}, u32[]{:S(2)}, u32[]{:S(2)}) collective-permute-start(bf16[1032,128]{1,0:T(8,128)(2,1)S(1)} %collective-permute-done.1.refs_4_), channel_id=1, source_target_pairs={{0,1},{1,0},{2,3},{3,2},{4,5},{5,4},{6,7},{7,6},{8,9},{9,8},{10,11... | collective-permute-start | bytes 792584 | tf_op jit(solution)/shard_map/ppermute | solution.py:247
  24.9 1.5 %collective-permute-start.6 = (bf16[1032,128]{1,0:T(8,128)(2,1)S(1)}, bf16[1032,128]{1,0:T(8,128)(2,1)S(1)}, u32[]{:S(2)}, u32[]{:S(2)}) collective-permute-start(bf16[1032,128]{1,0:T(8,128)(2,1)S(1)} %collective-permute-done.5.refs_5_), channel_id=1, source_target_pairs={{0,1},{1,0},{2,3},{3,2},{4,5},{5,4},{6,7},{7,6},{8,9},{9,8},{10,11... | collective-permute-start | bytes 792584 | tf_op jit(solution)/shard_map/ppermute | solution.py:247

commit v4 on v3

--- a/solution.py
+++ b/solution.py
@@ -164,12 +164,22 @@
         (q_ref, where_ref, mean_ref, level_ref), refs = refs[:4], refs[4:]
     block_refs, refs = refs[:shards], refs[shards:]
     if last:
-        out_hbm, bias_ref, weight_ref, out_ref, sems = refs
-        outs, stores = (out_ref,), []
+        out_hbm, bias_ref, out_ref, sems = refs
+        stores = []
     else:
-        outs, (bias_ref, weight_ref) = refs[:-2], refs[-2:]
+        outs, bias_ref = refs[:-1], refs[-1]
     rows = q_ref.shape[0]
     group = q_ref.shape[1] // HEAD_WIDTH // KEY_VALUE_HEADS
+
+    def raw_scores(head):
+        return lax.dot_general(
+            stacked(q_ref, head, group),
+            keys_of(block_refs, rows, head),
+            (((1,), (1,)), ((), ())),
+            preferred_element_type=jnp.float32,
+        )
+
+    raws = [raw_scores(0), raw_scores(1)]
     if first:
         square = (rows, rows)
         diagonal = lax.broadcasted_iota(jnp.int32, square, 0) == lax.broadcasted_iota(jnp.int32, square, 1)
@@ -186,18 +196,10 @@
         q_pos, q_first = where_ref[0], where_ref[1]
     write_bias(bias_ref, block_refs, q_pos, q_first)
 
-    for head in range(KEY_VALUE_HEADS):
-        k_part, v_part = keys_of(block_refs, rows, head), values_of(block_refs, rows, head)
-        raw = lax.dot_general(
-            stacked(q_ref, head, group),
-            k_part,
-            (((1,), (1,)), ((), ())),
-            preferred_element_type=jnp.float32,
-        )
-        tops, totals, before = [], [], []
+    def weigh(head):
+        weights, tops, totals, before = [], [], [], []
         for g in range(group):
-            part = slice(g * rows, (g + 1) * rows)
-            scores = raw[part] + bias_ref[...]
+            scores = raws[head][g * rows : (g + 1) * rows] + bias_ref[...]
             top = jnp.max(scores, axis=1, keepdims=True)
             if first:
                 weight = jnp.exp2((scores - top) * EXP2_SCALE)
@@ -208,10 +210,13 @@
                 weight = jnp.exp2((scores - jnp.tile(top, (1, shards))) * EXP2_SCALE)
                 before.append(jnp.exp2((level - top) * EXP2_SCALE))
                 total = before[-1] + jnp.sum(weight, axis=1, keepdims=True)
-            weight_ref[part] = weight.astype(jnp.bfloat16)
+            weights.append(weight.astype(jnp.bfloat16))
             tops.append(top)
             totals.append(total)
-        mixed = jnp.dot(weight_ref[...], v_part, preferred_element_type=jnp.float32)
+        return jnp.concatenate(weights, axis=0), tops, totals, before
+
+    def mix(head, weights, tops, totals, before):
+        mixed = jnp.dot(weights, values_of(block_refs, rows, head), preferred_element_type=jnp.float32)
         for g in range(group):
             q_head = head * group + g
             mean = mixed[g * rows : (g + 1) * rows]
@@ -219,7 +224,7 @@
                 mean = mean + before[g] * mean_ref[q_head]
             mean = mean * (1.0 / totals[g])
             if last:
-                outs[0][:, lanes(q_head)] = mean.astype(jnp.bfloat16)
+                out_ref[:, lanes(q_head)] = mean.astype(jnp.bfloat16)
             else:
                 outs[0][q_head] = mean
                 level = tops[g] + jnp.log2(totals[g]) * (1.0 / EXP2_SCALE)
@@ -230,6 +235,15 @@
                 pltpu.make_async_copy(out_ref.at[:, done], out_hbm.at[:, done], sems.at[head])
             )
             stores[-1].start()
+
+    weighed = []
+    for head in range(KEY_VALUE_HEADS):
+        weighed.append(weigh(head))
+        if head + 2 < KEY_VALUE_HEADS:
+            raws.append(raw_scores(head + 2))
+        if head > 0:
+            mix(head - 1, *weighed[head - 1])
+    mix(KEY_VALUE_HEADS - 1, *weighed[-1])
     if last:
         for store in stores:
             store.wait()
@@ -258,10 +272,7 @@
             out_shape=out_shape,
             in_specs=([smem] if first else []) + [vmem] * (1 + len(state) + n),
             out_specs=(hbm if last else vmem,) * len(out_shape),
-            scratch_shapes=[
-                pltpu.VMEM((rows, n * rows), jnp.float32),
-                pltpu.VMEM((heads // KEY_VALUE_HEADS * rows, n * rows), jnp.bfloat16),
-            ]
+            scratch_shapes=[pltpu.VMEM((rows, n * rows), jnp.float32)]
             + last
             * [
                 pltpu.VMEM(queries.shape, queries.dtype),
@@ -286,9 +297,9 @@
     six = swap(own, 6)
     two = swap(own, 2)
     four = swap(six, 2)
-    where, *state = fold("early", [own, six, two, swap(after(own, six), 1), swap(six, 1)])
+    where, *state = fold("early", [own, six, two, swap(own, 1)])
     four = after(four, *state)
-    state = fold("middle", [swap(two, 1), four], where, *state)
+    state = fold("middle", [swap(six, 1), swap(two, 1), four], where, *state)
     return fold("last", [swap(four, 1)], where, *state, last=True)[0]
 
 

time: 28.4 us -> 27.7 us (0.975)
  Pallas kernels: 7.46 us -> 6.94 us
  starting transfers between devices: 10.1 us -> 9.62 us
  waiting for transfers between devices: 10.6 us -> 10.9 us
    pallas_call x3, Pallas kernels: 6.44 us -> 5.92 us  [fold(): pl.pallas_call(lambda *refs: fold_kernel(n, first, last, *refs), out_shap...]
    ppermute x7, starting transfers between devices: 10.1 us -> 9.62 us  [swap(): return lax.ppermute(x, 'ctx', [(i, i ^ distance) for i in range(shards)])]
    ppermute x7, waiting for transfers between devices: 10.6 us -> 10.9 us  [swap(): return lax.ppermute(x, 'ctx', [(i, i ^ distance) for i in range(shards)])]
  transfers between devices with their start and end apart: 7 -> 7, of which waited for: 3 -> 3; matrix products, arithmetic and copies ran while one was open for 0% -> 0% of each run, Pallas kernels for 17% -> 15%
where the time goes in v4:
time: 27.7 us; the launch traced here: 27.5 us
  waiting for transfers between devices  10.9 us (39%)
  starting transfers between devices  9.62 us (35%)
  Pallas kernels  6.94 us (25%)
    ppermute x7, waiting for transfers between devices, swap(): return lax.ppermute(x, 'ctx', [(i, i ^ distance) for i in range(shards)])  10.9 us
    ppermute x7, starting transfers between devices, swap(): return lax.ppermute(x, 'ctx', [(i, i ^ distance) for i in range(shards)])  9.62 us
    pallas_call x3, Pallas kernels, fold(): pl.pallas_call(lambda *refs: fold_kernel(n, first, last, *refs), out_shap...  5.92 us
    pallas_call x1, Pallas kernels, gathered(): pl.pallas_call(pack_kernel, out_shape=pltpu.VMEM((slabs * rows + POS_ROWS...  1.03 us
  transfers between devices with their start and end apart: 7, of which 3 were waited for; matrix products, arithmetic and copies ran while one was open for 0% of the time, Pallas kernels for 15%

profile of v4, /device:TPU:0, one launch (start us, length us, event | category | flops | bytes accessed | tf_op | source)
XLA Modules:
  0.0 27.5 jit_solution(11496319197705479192)
XLA Ops:
  0.0 0.0 copy-start
  0.0 0.0 copy-start.1
  0.0 1.0 %pack.1.refs_2_ = bf16[1032,128]{1,0:T(8,128)(2,1)S(1)} custom-call(bf16[128,512]{1,0:T(8,128)(2,1)} %k_ref.1, bf16[128,512]{1,0:T(8,128)(2,1)} %v_ref.1, s32[1,128]{1,0:T(1,128)} %bitcast.1), custom_call_target="tpu_custom_call" | custom-call | tf_op jit(solution)/shard_map/pack/pallas_call | solution.py:286
  1.0 5.1 %collective-permute-start = (bf16[1032,128]{1,0:T(8,128)(2,1)S(1)}, bf16[1032,128]{1,0:T(8,128)(2,1)S(1)}, u32[]{:S(2)}, u32[]{:S(2)}) collective-permute-start(bf16[1032,128]{1,0:T(8,128)(2,1)S(1)} %pack.1.refs_2_), channel_id=1, source_target_pairs={{0,6},{1,7},{2,4},{3,5},{4,2},{5,3},{6,0},{7,1},{8,14},{9,15},{10,... | collective-permute-start | bytes 792584 | tf_op jit(solution)/shard_map/ppermute | solution.py:261
  6.2 0.0 collective-permute-start.1
  6.2 0.0 collective-permute-start.2
  6.2 7.3 %collective-permute-done.refs_3_ = bf16[1032,128]{1,0:T(8,128)(2,1)S(1)} collective-permute-done((bf16[1032,128]{1,0:T(8,128)(2,1)S(1)}, bf16[1032,128]{1,0:T(8,128)(2,1)S(1)}, u32[]{:S(2)}, u32[]{:S(2)}) %collective-permute-start) | collective-permute-done | bytes 264224 | tf_op jit(solution)/shard_map/ppermute | solution.py:261
  13.4 4.5 %collective-permute-start.5 = (bf16[1032,128]{1,0:T(8,128)(2,1)S(1)}, bf16[1032,128]{1,0:T(8,128)(2,1)S(1)}, u32[]{:S(2)}, u32[]{:S(2)}) collective-permute-start(bf16[1032,128]{1,0:T(8,128)(2,1)S(1)} %collective-permute-done.refs_3_), channel_id=1, source_target_pairs={{0,2},{1,3},{2,0},{3,1},{4,6},{5,7},{6,4},{7,5},{8,10},{9,11},{10,... | collective-permute-start | bytes 792584 | tf_op jit(solution)/shard_map/ppermute | solution.py:261
  17.9 0.0 collective-permute-start.3
  17.9 0.5 %collective-permute-done.1.refs_4_ = bf16[1032,128]{1,0:T(8,128)(2,1)S(1)} collective-permute-done((bf16[1032,128]{1,0:T(8,128)(2,1)S(1)}, bf16[1032,128]{1,0:T(8,128)(2,1)S(1)}, u32[]{:S(2)}, u32[]{:S(2)}) %collective-permute-start.1) | collective-permute-done | bytes 264224 | tf_op jit(solution)/shard_map/ppermute | solution.py:261
  18.4 0.0 collective-permute-start.4
  18.4 0.0 collective-permute-done.2.refs_5_
  18.4 0.0 copy-done
  18.4 0.0 copy-done.1
  18.4 2.3 %early.1 = (f32[2,128,128]{2,1,0:T(8,128)S(1)}, f32[16,128,128]{2,1,0:T(8,128)S(1)}, f32[16,128,128]{2,1,0:T(8,128)S(1)}) custom-call(s32[8]{0:T(128)S(1)} %copy-done.1, bf16[128,2048]{1,0:T(8,128)(2,1)S(1)} %copy-done, bf16[1032,128]{1,0:T(8,128)(2,1)S(1)} %pack.1.refs_2_, bf16[1032,128]{1,0:T(8,128)(2,1)S(1)} %collective-permute-done.refs_3_, ...), custom_call_target="tpu_custom_call" | custom-call | tf_op jit(solution)/shard_map/early/pallas_call | solution.py:270
  20.8 3.2 %collective-permute-done.5.refs_6_ = bf16[1032,128]{1,0:T(8,128)(2,1)S(1)} collective-permute-done((bf16[1032,128]{1,0:T(8,128)(2,1)S(1)}, bf16[1032,128]{1,0:T(8,128)(2,1)S(1)}, u32[]{:S(2)}, u32[]{:S(2)}) %collective-permute-start.5) | collective-permute-done | bytes 264224 | tf_op jit(solution)/shard_map/ppermute | solution.py:261
  23.9 0.0 collective-permute-start.6
  23.9 0.0 collective-permute-done.4.refs_5_
  23.9 0.0 collective-permute-done.3.refs_4_
  23.9 1.9 %middle.1 = (f32[16,128,128]{2,1,0:T(8,128)S(1)}, f32[16,128,128]{2,1,0:T(8,128)S(1)}) custom-call(bf16[128,2048]{1,0:T(8,128)(2,1)S(1)} %copy-done, f32[2,128,128]{2,1,0:T(8,128)S(1)} %get-tuple-element.11.refs_1_, f32[16,128,128]{2,1,0:T(8,128)S(1)} %get-tuple-element.12.refs_2_, f32[16,128,128]{2,1,0:T(8,128)S(1)} %get-tuple-element.13.refs_3_, ...), custom_call_target="tpu_custom_call" | custom-call | tf_op jit(solution)/shard_map/middle/pallas_call | solution.py:270
  25.8 0.0 collective-permute-done.6.refs_4_
  25.8 1.7 %last.1 = bf16[128,2048]{1,0:T(8,128)(2,1)} custom-call(bf16[128,2048]{1,0:T(8,128)(2,1)S(1)} %copy-done, f32[2,128,128]{2,1,0:T(8,128)S(1)} %get-tuple-element.11.refs_1_, f32[16,128,128]{2,1,0:T(8,128)S(1)} %get-tuple-element.15.refs_2_, f32[16,128,128]{2,1,0:T(8,128)S(1)} %get-tuple-element.16.refs_3_, bf16[1032,128]{1,0:T(8,128)(2,1)S(1)} %collective-permute-done.6.refs_4_), custom_call_target="tpu_custom_call" | custom-call | tf_op jit(solution)/shard_map/last/pallas_call | solution.py:270
Async XLA Ops:
  0.0 18.4 %copy-start = (bf16[128,2048]{1,0:T(8,128)(2,1)S(1)}, bf16[128,2048]{1,0:T(8,128)(2,1)}, u32[]{:S(2)}) copy-start(bf16[128,2048]{1,0:T(8,128)(2,1)} %refs_0_.5) | copy-start | bytes 1572868
  0.0 18.4 %copy-start.1 = (s32[8]{0:T(128)S(1)}, s32[8]{0:T(128)}, u32[]{:S(2)}) copy-start(s32[8]{0:T(128)} %refs_0_.3) | copy-start | bytes 100
  1.0 12.4 %collective-permute-start = (bf16[1032,128]{1,0:T(8,128)(2,1)S(1)}, bf16[1032,128]{1,0:T(8,128)(2,1)S(1)}, u32[]{:S(2)}, u32[]{:S(2)}) collective-permute-start(bf16[1032,128]{1,0:T(8,128)(2,1)S(1)} %pack.1.refs_2_), channel_id=1, source_target_pairs={{0,6},{1,7},{2,4},{3,5},{4,2},{5,3},{6,0},{7,1},{8,14},{9,15},{10,... | collective-permute-start | bytes 792584 | tf_op jit(solution)/shard_map/ppermute | solution.py:261
  6.2 12.2 %collective-permute-start.1 = (bf16[1032,128]{1,0:T(8,128)(2,1)S(1)}, bf16[1032,128]{1,0:T(8,128)(2,1)S(1)}, u32[]{:S(2)}, u32[]{:S(2)}) collective-permute-start(bf16[1032,128]{1,0:T(8,128)(2,1)S(1)} %pack.1.refs_2_), channel_id=1, source_target_pairs={{0,2},{1,3},{2,0},{3,1},{4,6},{5,7},{6,4},{7,5},{8,10},{9,11},{10,... | collective-permute-start | bytes 792584 | tf_op jit(solution)/shard_map/ppermute | solution.py:261
  6.2 12.2 %collective-permute-start.2 = (bf16[1032,128]{1,0:T(8,128)(2,1)S(1)}, bf16[1032,128]{1,0:T(8,128)(2,1)S(1)}, u32[]{:S(2)}, u32[]{:S(2)}) collective-permute-start(bf16[1032,128]{1,0:T(8,128)(2,1)S(1)} %pack.1.refs_2_), channel_id=1, source_target_pairs={{0,1},{1,0},{2,3},{3,2},{4,5},{5,4},{6,7},{7,6},{8,9},{9,8},{10,11... | collective-permute-start | bytes 792584 | tf_op jit(solution)/shard_map/ppermute | solution.py:261
  13.4 10.5 %collective-permute-start.5 = (bf16[1032,128]{1,0:T(8,128)(2,1)S(1)}, bf16[1032,128]{1,0:T(8,128)(2,1)S(1)}, u32[]{:S(2)}, u32[]{:S(2)}) collective-permute-start(bf16[1032,128]{1,0:T(8,128)(2,1)S(1)} %collective-permute-done.refs_3_), channel_id=1, source_target_pairs={{0,2},{1,3},{2,0},{3,1},{4,6},{5,7},{6,4},{7,5},{8,10},{9,11},{10,... | collective-permute-start | bytes 792584 | tf_op jit(solution)/shard_map/ppermute | solution.py:261
  17.9 6.1 %collective-permute-start.3 = (bf16[1032,128]{1,0:T(8,128)(2,1)S(1)}, bf16[1032,128]{1,0:T(8,128)(2,1)S(1)}, u32[]{:S(2)}, u32[]{:S(2)}) collective-permute-start(bf16[1032,128]{1,0:T(8,128)(2,1)S(1)} %collective-permute-done.refs_3_), channel_id=1, source_target_pairs={{0,1},{1,0},{2,3},{3,2},{4,5},{5,4},{6,7},{7,6},{8,9},{9,8},{10,11... | collective-permute-start | bytes 792584 | tf_op jit(solution)/shard_map/ppermute | solution.py:261
  18.4 5.6 %collective-permute-start.4 = (bf16[1032,128]{1,0:T(8,128)(2,1)S(1)}, bf16[1032,128]{1,0:T(8,128)(2,1)S(1)}, u32[]{:S(2)}, u32[]{:S(2)}) collective-permute-start(bf16[1032,128]{1,0:T(8,128)(2,1)S(1)} %collective-permute-done.1.refs_4_), channel_id=1, source_target_pairs={{0,1},{1,0},{2,3},{3,2},{4,5},{5,4},{6,7},{7,6},{8,9},{9,8},{10,11... | collective-permute-start | bytes 792584 | tf_op jit(solution)/shard_map/ppermute | solution.py:261
  23.9 1.9 %collective-permute-start.6 = (bf16[1032,128]{1,0:T(8,128)(2,1)S(1)}, bf16[1032,128]{1,0:T(8,128)(2,1)S(1)}, u32[]{:S(2)}, u32[]{:S(2)}) collective-permute-start(bf16[1032,128]{1,0:T(8,128)(2,1)S(1)} %collective-permute-done.5.refs_6_), channel_id=1, source_target_pairs={{0,1},{1,0},{2,3},{3,2},{4,5},{5,4},{6,7},{7,6},{8,9},{9,8},{10,11... | collective-permute-start | bytes 792584 | tf_op jit(solution)/shard_map/ppermute | solution.py:261

commit v5 on v4

--- a/solution.py
+++ b/solution.py
@@ -161,7 +161,7 @@
     if first:
         (doc_ref, q_ref), refs = refs[:2], refs[2:]
     else:
-        (q_ref, where_ref, mean_ref, level_ref), refs = refs[:4], refs[4:]
+        (q_ref, where_ref, sum_ref, top_ref, total_ref), refs = refs[:5], refs[5:]
     block_refs, refs = refs[:shards], refs[shards:]
     if last:
         out_hbm, bias_ref, out_ref, sems = refs
@@ -205,11 +205,12 @@
                 weight = jnp.exp2((scores - top) * EXP2_SCALE)
                 total = jnp.sum(weight, axis=1, keepdims=True)
             else:
-                level = level_ref[head * group + g]
-                top = jnp.maximum(top, level)
+                old_top = top_ref[head * group + g]
+                top = jnp.maximum(top, old_top)
                 weight = jnp.exp2((scores - jnp.tile(top, (1, shards))) * EXP2_SCALE)
-                before.append(jnp.exp2((level - top) * EXP2_SCALE))
-                total = before[-1] + jnp.sum(weight, axis=1, keepdims=True)
+                before.append(jnp.exp2((old_top - top) * EXP2_SCALE))
+                total = jnp.sum(weight, axis=1, keepdims=True)
+                total = before[-1] * total_ref[head * group + g] + total
             weights.append(weight.astype(jnp.bfloat16))
             tops.append(top)
             totals.append(total)
@@ -219,16 +220,15 @@
         mixed = jnp.dot(weights, values_of(block_refs, rows, head), preferred_element_type=jnp.float32)
         for g in range(group):
             q_head = head * group + g
-            mean = mixed[g * rows : (g + 1) * rows]
+            found = mixed[g * rows : (g + 1) * rows]
             if not first:
-                mean = mean + before[g] * mean_ref[q_head]
-            mean = mean * (1.0 / totals[g])
+                found = found + before[g] * sum_ref[q_head]
             if last:
-                out_ref[:, lanes(q_head)] = mean.astype(jnp.bfloat16)
+                out_ref[:, lanes(q_head)] = (found * (1.0 / totals[g])).astype(jnp.bfloat16)
             else:
-                outs[0][q_head] = mean
-                level = tops[g] + jnp.log2(totals[g]) * (1.0 / EXP2_SCALE)
-                outs[1][q_head] = jnp.broadcast_to(level, (rows, HEAD_WIDTH))
+                outs[0][q_head] = found
+                outs[1][q_head] = jnp.broadcast_to(tops[g], (rows, HEAD_WIDTH))
+                outs[2][q_head] = jnp.broadcast_to(totals[g], (rows, HEAD_WIDTH))
         if last:
             done = slice(head * group * HEAD_WIDTH, (head + 1) * group * HEAD_WIDTH)
             stores.append(
@@ -262,7 +262,7 @@
 
     def fold(name, blocks, *state, last=False):
         n, first = len(blocks), not state
-        out_shape = (per_head, per_head)
+        out_shape = (per_head, per_head, per_head)
         if first:
             out_shape = (jax.ShapeDtypeStruct((2, rows, HEAD_WIDTH), jnp.float32), *out_shape)
         if last:

time: 27.7 us -> 27.7 us (level)
  no operation moved by 1% of the time
where the time goes in v5:
time: 27.7 us; the launch traced here: 27.6 us
  waiting for transfers between devices  11 us (40%)
  starting transfers between devices  9.62 us (35%)
  Pallas kernels  6.91 us (25%)
    ppermute x7, waiting for transfers between devices, swap(): return lax.ppermute(x, 'ctx', [(i, i ^ distance) for i in range(shards)])  11 us
    ppermute x7, starting transfers between devices, swap(): return lax.ppermute(x, 'ctx', [(i, i ^ distance) for i in range(shards)])  9.62 us
    pallas_call x3, Pallas kernels, fold(): pl.pallas_call(lambda *refs: fold_kernel(n, first, last, *refs), out_shap...  5.88 us
    pallas_call x1, Pallas kernels, gathered(): pl.pallas_call(pack_kernel, out_shape=pltpu.VMEM((slabs * rows + POS_ROWS...  1.03 us
  transfers between devices with their start and end apart: 7, of which 3 were waited for; matrix products, arithmetic and copies ran while one was open for 0% of the time, Pallas kernels for 15%

profile of v5, /device:TPU:0, one launch (start us, length us, event | category | flops | bytes accessed | tf_op | source)
XLA Modules:
  0.0 27.6 jit_solution(8189133416737629534)
XLA Ops:
  0.0 0.0 copy-start
  0.0 0.0 copy-start.1
  0.0 1.0 %pack.1.refs_2_ = bf16[1032,128]{1,0:T(8,128)(2,1)S(1)} custom-call(bf16[128,512]{1,0:T(8,128)(2,1)} %k_ref.1, bf16[128,512]{1,0:T(8,128)(2,1)} %v_ref.1, s32[1,128]{1,0:T(1,128)} %bitcast.1), custom_call_target="tpu_custom_call" | custom-call | tf_op jit(solution)/shard_map/pack/pallas_call | solution.py:286
  1.0 5.1 %collective-permute-start = (bf16[1032,128]{1,0:T(8,128)(2,1)S(1)}, bf16[1032,128]{1,0:T(8,128)(2,1)S(1)}, u32[]{:S(2)}, u32[]{:S(2)}) collective-permute-start(bf16[1032,128]{1,0:T(8,128)(2,1)S(1)} %pack.1.refs_2_), channel_id=1, source_target_pairs={{0,6},{1,7},{2,4},{3,5},{4,2},{5,3},{6,0},{7,1},{8,14},{9,15},{10,... | collective-permute-start | bytes 792584 | tf_op jit(solution)/shard_map/ppermute | solution.py:261
  6.2 0.0 collective-permute-start.1
  6.2 0.0 collective-permute-start.2
  6.2 7.3 %collective-permute-done.refs_3_ = bf16[1032,128]{1,0:T(8,128)(2,1)S(1)} collective-permute-done((bf16[1032,128]{1,0:T(8,128)(2,1)S(1)}, bf16[1032,128]{1,0:T(8,128)(2,1)S(1)}, u32[]{:S(2)}, u32[]{:S(2)}) %collective-permute-start) | collective-permute-done | bytes 264224 | tf_op jit(solution)/shard_map/ppermute | solution.py:261
  13.4 4.5 %collective-permute-start.5 = (bf16[1032,128]{1,0:T(8,128)(2,1)S(1)}, bf16[1032,128]{1,0:T(8,128)(2,1)S(1)}, u32[]{:S(2)}, u32[]{:S(2)}) collective-permute-start(bf16[1032,128]{1,0:T(8,128)(2,1)S(1)} %collective-permute-done.refs_3_), channel_id=1, source_target_pairs={{0,2},{1,3},{2,0},{3,1},{4,6},{5,7},{6,4},{7,5},{8,10},{9,11},{10,... | collective-permute-start | bytes 792584 | tf_op jit(solution)/shard_map/ppermute | solution.py:261
  17.9 0.0 collective-permute-start.3
  17.9 0.5 %collective-permute-done.1.refs_4_ = bf16[1032,128]{1,0:T(8,128)(2,1)S(1)} collective-permute-done((bf16[1032,128]{1,0:T(8,128)(2,1)S(1)}, bf16[1032,128]{1,0:T(8,128)(2,1)S(1)}, u32[]{:S(2)}, u32[]{:S(2)}) %collective-permute-start.1) | collective-permute-done | bytes 264224 | tf_op jit(solution)/shard_map/ppermute | solution.py:261
  18.4 0.0 collective-permute-start.4
  18.4 0.0 collective-permute-done.2.refs_5_
  18.4 0.0 copy-done
  18.4 0.0 copy-done.1
  18.4 2.3 %early.1 = (f32[2,128,128]{2,1,0:T(8,128)S(1)}, f32[16,128,128]{2,1,0:T(8,128)S(1)}, f32[16,128,128]{2,1,0:T(8,128)S(1)}, f32[16,128,128]{2,1,0:T(8,128)S(1)}) custom-call(s32[8]{0:T(128)S(1)} %copy-done.1, bf16[128,2048]{1,0:T(8,128)(2,1)S(1)} %copy-done, bf16[1032,128]{1,0:T(8,128)(2,1)S(1)} %pack.1.refs_2_, ...), custom_call_target="tpu_custom_call" | custom-call | tf_op jit(solution)/shard_map/early/pallas_call | solution.py:270
  20.7 3.2 %collective-permute-done.5.refs_7_ = bf16[1032,128]{1,0:T(8,128)(2,1)S(1)} collective-permute-done((bf16[1032,128]{1,0:T(8,128)(2,1)S(1)}, bf16[1032,128]{1,0:T(8,128)(2,1)S(1)}, u32[]{:S(2)}, u32[]{:S(2)}) %collective-permute-start.5) | collective-permute-done | bytes 264224 | tf_op jit(solution)/shard_map/ppermute | solution.py:261
  23.9 0.0 collective-permute-start.6
  23.9 0.0 collective-permute-done.4.refs_6_
  23.9 0.0 collective-permute-done.3.refs_5_
  23.9 1.9 %middle.1 = (f32[16,128,128]{2,1,0:T(8,128)S(1)}, f32[16,128,128]{2,1,0:T(8,128)S(1)}, f32[16,128,128]{2,1,0:T(8,128)S(1)}) custom-call(bf16[128,2048]{1,0:T(8,128)(2,1)S(1)} %copy-done, f32[2,128,128]{2,1,0:T(8,128)S(1)} %get-tuple-element.13.refs_1_, f32[16,128,128]{2,1,0:T(8,128)S(1)} %get-tuple-element.14.refs_2_, ...), custom_call_target="tpu_custom_call" | custom-call | tf_op jit(solution)/shard_map/middle/pallas_call | solution.py:270
  25.8 0.0 collective-permute-done.6.refs_5_
  25.8 1.7 %last.1 = bf16[128,2048]{1,0:T(8,128)(2,1)} custom-call(bf16[128,2048]{1,0:T(8,128)(2,1)S(1)} %copy-done, f32[2,128,128]{2,1,0:T(8,128)S(1)} %get-tuple-element.13.refs_1_, f32[16,128,128]{2,1,0:T(8,128)S(1)} %get-tuple-element.18.refs_2_, f32[16,128,128]{2,1,0:T(8,128)S(1)} %get-tuple-element.19.refs_3_, f32[16,128,128]{2,1,0:T(8,128)S(1)} %get-tuple-element.20.refs_4_, ...), custom_call_target="tpu_custom_call" | custom-call | tf_op jit(solution)/shard_map/last/pallas_call | solution.py:270
Async XLA Ops:
  0.0 18.4 %copy-start = (bf16[128,2048]{1,0:T(8,128)(2,1)S(1)}, bf16[128,2048]{1,0:T(8,128)(2,1)}, u32[]{:S(2)}) copy-start(bf16[128,2048]{1,0:T(8,128)(2,1)} %refs_0_.5) | copy-start | bytes 1572868
  0.0 18.4 %copy-start.1 = (s32[8]{0:T(128)S(1)}, s32[8]{0:T(128)}, u32[]{:S(2)}) copy-start(s32[8]{0:T(128)} %refs_0_.3) | copy-start | bytes 100
  1.0 12.4 %collective-permute-start = (bf16[1032,128]{1,0:T(8,128)(2,1)S(1)}, bf16[1032,128]{1,0:T(8,128)(2,1)S(1)}, u32[]{:S(2)}, u32[]{:S(2)}) collective-permute-start(bf16[1032,128]{1,0:T(8,128)(2,1)S(1)} %pack.1.refs_2_), channel_id=1, source_target_pairs={{0,6},{1,7},{2,4},{3,5},{4,2},{5,3},{6,0},{7,1},{8,14},{9,15},{10,... | collective-permute-start | bytes 792584 | tf_op jit(solution)/shard_map/ppermute | solution.py:261
  6.2 12.2 %collective-permute-start.1 = (bf16[1032,128]{1,0:T(8,128)(2,1)S(1)}, bf16[1032,128]{1,0:T(8,128)(2,1)S(1)}, u32[]{:S(2)}, u32[]{:S(2)}) collective-permute-start(bf16[1032,128]{1,0:T(8,128)(2,1)S(1)} %pack.1.refs_2_), channel_id=1, source_target_pairs={{0,2},{1,3},{2,0},{3,1},{4,6},{5,7},{6,4},{7,5},{8,10},{9,11},{10,... | collective-permute-start | bytes 792584 | tf_op jit(solution)/shard_map/ppermute | solution.py:261
  6.2 12.2 %collective-permute-start.2 = (bf16[1032,128]{1,0:T(8,128)(2,1)S(1)}, bf16[1032,128]{1,0:T(8,128)(2,1)S(1)}, u32[]{:S(2)}, u32[]{:S(2)}) collective-permute-start(bf16[1032,128]{1,0:T(8,128)(2,1)S(1)} %pack.1.refs_2_), channel_id=1, source_target_pairs={{0,1},{1,0},{2,3},{3,2},{4,5},{5,4},{6,7},{7,6},{8,9},{9,8},{10,11... | collective-permute-start | bytes 792584 | tf_op jit(solution)/shard_map/ppermute | solution.py:261
  13.4 10.5 %collective-permute-start.5 = (bf16[1032,128]{1,0:T(8,128)(2,1)S(1)}, bf16[1032,128]{1,0:T(8,128)(2,1)S(1)}, u32[]{:S(2)}, u32[]{:S(2)}) collective-permute-start(bf16[1032,128]{1,0:T(8,128)(2,1)S(1)} %collective-permute-done.refs_3_), channel_id=1, source_target_pairs={{0,2},{1,3},{2,0},{3,1},{4,6},{5,7},{6,4},{7,5},{8,10},{9,11},{10,... | collective-permute-start | bytes 792584 | tf_op jit(solution)/shard_map/ppermute | solution.py:261
  17.9 6.1 %collective-permute-start.3 = (bf16[1032,128]{1,0:T(8,128)(2,1)S(1)}, bf16[1032,128]{1,0:T(8,128)(2,1)S(1)}, u32[]{:S(2)}, u32[]{:S(2)}) collective-permute-start(bf16[1032,128]{1,0:T(8,128)(2,1)S(1)} %collective-permute-done.refs_3_), channel_id=1, source_target_pairs={{0,1},{1,0},{2,3},{3,2},{4,5},{5,4},{6,7},{7,6},{8,9},{9,8},{10,11... | collective-permute-start | bytes 792584 | tf_op jit(solution)/shard_map/ppermute | solution.py:261
  18.4 5.6 %collective-permute-start.4 = (bf16[1032,128]{1,0:T(8,128)(2,1)S(1)}, bf16[1032,128]{1,0:T(8,128)(2,1)S(1)}, u32[]{:S(2)}, u32[]{:S(2)}) collective-permute-start(bf16[1032,128]{1,0:T(8,128)(2,1)S(1)} %collective-permute-done.1.refs_4_), channel_id=1, source_target_pairs={{0,1},{1,0},{2,3},{3,2},{4,5},{5,4},{6,7},{7,6},{8,9},{9,8},{10,11... | collective-permute-start | bytes 792584 | tf_op jit(solution)/shard_map/ppermute | solution.py:261
  23.9 1.9 %collective-permute-start.6 = (bf16[1032,128]{1,0:T(8,128)(2,1)S(1)}, bf16[1032,128]{1,0:T(8,128)(2,1)S(1)}, u32[]{:S(2)}, u32[]{:S(2)}) collective-permute-start(bf16[1032,128]{1,0:T(8,128)(2,1)S(1)} %collective-permute-done.5.refs_7_), channel_id=1, source_target_pairs={{0,1},{1,0},{2,3},{3,2},{4,5},{5,4},{6,7},{7,6},{8,9},{9,8},{10,11... | collective-permute-start | bytes 792584 | tf_op jit(solution)/shard_map/ppermute | solution.py:261

commit v6 on v5

--- a/solution.py
+++ b/solution.py
@@ -157,6 +157,10 @@
     return jnp.concatenate([ref[:, lanes(head * group + g)] for g in range(group)], axis=0)
 
 
+def lane_sums(weight):
+    return sum(weight[:, lanes(i)] for i in range(weight.shape[1] // HEAD_WIDTH))
+
+
 def fold_kernel(shards, first, last, *refs):
     if first:
         (doc_ref, q_ref), refs = refs[:2], refs[2:]
@@ -203,14 +207,15 @@
             top = jnp.max(scores, axis=1, keepdims=True)
             if first:
                 weight = jnp.exp2((scores - top) * EXP2_SCALE)
-                total = jnp.sum(weight, axis=1, keepdims=True)
+                total = lane_sums(weight)
             else:
                 old_top = top_ref[head * group + g]
                 top = jnp.maximum(top, old_top)
                 weight = jnp.exp2((scores - jnp.tile(top, (1, shards))) * EXP2_SCALE)
                 before.append(jnp.exp2((old_top - top) * EXP2_SCALE))
-                total = jnp.sum(weight, axis=1, keepdims=True)
-                total = before[-1] * total_ref[head * group + g] + total
+                total = before[-1] * total_ref[head * group + g] + lane_sums(weight)
+                if last:
+                    total = jnp.sum(total, axis=1, keepdims=True)
             weights.append(weight.astype(jnp.bfloat16))
             tops.append(top)
             totals.append(total)
@@ -228,7 +233,7 @@
             else:
                 outs[0][q_head] = found
                 outs[1][q_head] = jnp.broadcast_to(tops[g], (rows, HEAD_WIDTH))
-                outs[2][q_head] = jnp.broadcast_to(totals[g], (rows, HEAD_WIDTH))
+                outs[2][q_head] = totals[g]
         if last:
             done = slice(head * group * HEAD_WIDTH, (head + 1) * group * HEAD_WIDTH)
             stores.append(

time: 27.7 us -> 27.5 us (level)
  no operation moved by 1% of the time
where the time goes in v6:
time: 27.5 us; the launch traced here: 27.3 us
  waiting for transfers between devices  10.9 us (40%)
  starting transfers between devices  9.62 us (35%)
  Pallas kernels  6.78 us (25%)
    ppermute x7, waiting for transfers between devices, swap(): return lax.ppermute(x, 'ctx', [(i, i ^ distance) for i in range(shards)])  10.9 us
    ppermute x7, starting transfers between devices, swap(): return lax.ppermute(x, 'ctx', [(i, i ^ distance) for i in range(shards)])  9.62 us
    pallas_call x3, Pallas kernels, fold(): pl.pallas_call(lambda *refs: fold_kernel(n, first, last, *refs), out_shap...  5.76 us
    pallas_call x1, Pallas kernels, gathered(): pl.pallas_call(pack_kernel, out_shape=pltpu.VMEM((slabs * rows + POS_ROWS...  1.03 us
  transfers between devices with their start and end apart: 7, of which 3 were waited for; matrix products, arithmetic and copies ran while one was open for 0% of the time, Pallas kernels for 15%

profile of v6, /device:TPU:0, one launch (start us, length us, event | category | flops | bytes accessed | tf_op | source)
XLA Modules:
  0.0 27.3 jit_solution(12375571206024272640)
XLA Ops:
  0.0 0.0 copy-start
  0.0 0.0 copy-start.1
  0.0 1.0 %pack.1.refs_2_ = bf16[1032,128]{1,0:T(8,128)(2,1)S(1)} custom-call(bf16[128,512]{1,0:T(8,128)(2,1)} %k_ref.1, bf16[128,512]{1,0:T(8,128)(2,1)} %v_ref.1, s32[1,128]{1,0:T(1,128)} %bitcast.1), custom_call_target="tpu_custom_call" | custom-call | tf_op jit(solution)/shard_map/pack/pallas_call | solution.py:291
  1.0 5.1 %collective-permute-start = (bf16[1032,128]{1,0:T(8,128)(2,1)S(1)}, bf16[1032,128]{1,0:T(8,128)(2,1)S(1)}, u32[]{:S(2)}, u32[]{:S(2)}) collective-permute-start(bf16[1032,128]{1,0:T(8,128)(2,1)S(1)} %pack.1.refs_2_), channel_id=1, source_target_pairs={{0,6},{1,7},{2,4},{3,5},{4,2},{5,3},{6,0},{7,1},{8,14},{9,15},{10,... | collective-permute-start | bytes 792584 | tf_op jit(solution)/shard_map/ppermute | solution.py:266
  6.2 0.0 collective-permute-start.1
  6.2 0.0 collective-permute-start.2
  6.2 7.3 %collective-permute-done.refs_3_ = bf16[1032,128]{1,0:T(8,128)(2,1)S(1)} collective-permute-done((bf16[1032,128]{1,0:T(8,128)(2,1)S(1)}, bf16[1032,128]{1,0:T(8,128)(2,1)S(1)}, u32[]{:S(2)}, u32[]{:S(2)}) %collective-permute-start) | collective-permute-done | bytes 264224 | tf_op jit(solution)/shard_map/ppermute | solution.py:266
  13.4 4.5 %collective-permute-start.5 = (bf16[1032,128]{1,0:T(8,128)(2,1)S(1)}, bf16[1032,128]{1,0:T(8,128)(2,1)S(1)}, u32[]{:S(2)}, u32[]{:S(2)}) collective-permute-start(bf16[1032,128]{1,0:T(8,128)(2,1)S(1)} %collective-permute-done.refs_3_), channel_id=1, source_target_pairs={{0,2},{1,3},{2,0},{3,1},{4,6},{5,7},{6,4},{7,5},{8,10},{9,11},{10,... | collective-permute-start | bytes 792584 | tf_op jit(solution)/shard_map/ppermute | solution.py:266
  17.9 0.0 collective-permute-start.3
  17.9 0.5 %collective-permute-done.1.refs_4_ = bf16[1032,128]{1,0:T(8,128)(2,1)S(1)} collective-permute-done((bf16[1032,128]{1,0:T(8,128)(2,1)S(1)}, bf16[1032,128]{1,0:T(8,128)(2,1)S(1)}, u32[]{:S(2)}, u32[]{:S(2)}) %collective-permute-start.1) | collective-permute-done | bytes 264224 | tf_op jit(solution)/shard_map/ppermute | solution.py:266
  18.4 0.0 collective-permute-start.4
  18.4 0.0 collective-permute-done.2.refs_5_
  18.4 0.0 copy-done
  18.4 0.0 copy-done.1
  18.4 2.4 %early.1 = (f32[2,128,128]{2,1,0:T(8,128)S(1)}, f32[16,128,128]{2,1,0:T(8,128)S(1)}, f32[16,128,128]{2,1,0:T(8,128)S(1)}, f32[16,128,128]{2,1,0:T(8,128)S(1)}) custom-call(s32[8]{0:T(128)S(1)} %copy-done.1, bf16[128,2048]{1,0:T(8,128)(2,1)S(1)} %copy-done, bf16[1032,128]{1,0:T(8,128)(2,1)S(1)} %pack.1.refs_2_, ...), custom_call_target="tpu_custom_call" | custom-call | tf_op jit(solution)/shard_map/early/pallas_call | solution.py:275
  20.8 3.1 %collective-permute-done.5.refs_7_ = bf16[1032,128]{1,0:T(8,128)(2,1)S(1)} collective-permute-done((bf16[1032,128]{1,0:T(8,128)(2,1)S(1)}, bf16[1032,128]{1,0:T(8,128)(2,1)S(1)}, u32[]{:S(2)}, u32[]{:S(2)}) %collective-permute-start.5) | collective-permute-done | bytes 264224 | tf_op jit(solution)/shard_map/ppermute | solution.py:266
  23.9 0.0 collective-permute-start.6
  23.9 0.0 collective-permute-done.4.refs_6_
  23.9 0.0 collective-permute-done.3.refs_5_
  23.9 1.7 %middle.1 = (f32[16,128,128]{2,1,0:T(8,128)S(1)}, f32[16,128,128]{2,1,0:T(8,128)S(1)}, f32[16,128,128]{2,1,0:T(8,128)S(1)}) custom-call(bf16[128,2048]{1,0:T(8,128)(2,1)S(1)} %copy-done, f32[2,128,128]{2,1,0:T(8,128)S(1)} %get-tuple-element.13.refs_1_, f32[16,128,128]{2,1,0:T(8,128)S(1)} %get-tuple-element.14.refs_2_, ...), custom_call_target="tpu_custom_call" | custom-call | tf_op jit(solution)/shard_map/middle/pallas_call | solution.py:275
  25.6 0.0 collective-permute-done.6.refs_5_
  25.6 1.7 %last.1 = bf16[128,2048]{1,0:T(8,128)(2,1)} custom-call(bf16[128,2048]{1,0:T(8,128)(2,1)S(1)} %copy-done, f32[2,128,128]{2,1,0:T(8,128)S(1)} %get-tuple-element.13.refs_1_, f32[16,128,128]{2,1,0:T(8,128)S(1)} %get-tuple-element.18.refs_2_, f32[16,128,128]{2,1,0:T(8,128)S(1)} %get-tuple-element.19.refs_3_, f32[16,128,128]{2,1,0:T(8,128)S(1)} %get-tuple-element.20.refs_4_, ...), custom_call_target="tpu_custom_call" | custom-call | tf_op jit(solution)/shard_map/last/pallas_call | solution.py:275
Async XLA Ops:
  0.0 18.4 %copy-start = (bf16[128,2048]{1,0:T(8,128)(2,1)S(1)}, bf16[128,2048]{1,0:T(8,128)(2,1)}, u32[]{:S(2)}) copy-start(bf16[128,2048]{1,0:T(8,128)(2,1)} %refs_0_.5) | copy-start | bytes 1572868
  0.0 18.4 %copy-start.1 = (s32[8]{0:T(128)S(1)}, s32[8]{0:T(128)}, u32[]{:S(2)}) copy-start(s32[8]{0:T(128)} %refs_0_.3) | copy-start | bytes 100
  1.0 12.4 %collective-permute-start = (bf16[1032,128]{1,0:T(8,128)(2,1)S(1)}, bf16[1032,128]{1,0:T(8,128)(2,1)S(1)}, u32[]{:S(2)}, u32[]{:S(2)}) collective-permute-start(bf16[1032,128]{1,0:T(8,128)(2,1)S(1)} %pack.1.refs_2_), channel_id=1, source_target_pairs={{0,6},{1,7},{2,4},{3,5},{4,2},{5,3},{6,0},{7,1},{8,14},{9,15},{10,... | collective-permute-start | bytes 792584 | tf_op jit(solution)/shard_map/ppermute | solution.py:266
  6.2 12.2 %collective-permute-start.1 = (bf16[1032,128]{1,0:T(8,128)(2,1)S(1)}, bf16[1032,128]{1,0:T(8,128)(2,1)S(1)}, u32[]{:S(2)}, u32[]{:S(2)}) collective-permute-start(bf16[1032,128]{1,0:T(8,128)(2,1)S(1)} %pack.1.refs_2_), channel_id=1, source_target_pairs={{0,2},{1,3},{2,0},{3,1},{4,6},{5,7},{6,4},{7,5},{8,10},{9,11},{10,... | collective-permute-start | bytes 792584 | tf_op jit(solution)/shard_map/ppermute | solution.py:266
  6.2 12.2 %collective-permute-start.2 = (bf16[1032,128]{1,0:T(8,128)(2,1)S(1)}, bf16[1032,128]{1,0:T(8,128)(2,1)S(1)}, u32[]{:S(2)}, u32[]{:S(2)}) collective-permute-start(bf16[1032,128]{1,0:T(8,128)(2,1)S(1)} %pack.1.refs_2_), channel_id=1, source_target_pairs={{0,1},{1,0},{2,3},{3,2},{4,5},{5,4},{6,7},{7,6},{8,9},{9,8},{10,11... | collective-permute-start | bytes 792584 | tf_op jit(solution)/shard_map/ppermute | solution.py:266
  13.4 10.5 %collective-permute-start.5 = (bf16[1032,128]{1,0:T(8,128)(2,1)S(1)}, bf16[1032,128]{1,0:T(8,128)(2,1)S(1)}, u32[]{:S(2)}, u32[]{:S(2)}) collective-permute-start(bf16[1032,128]{1,0:T(8,128)(2,1)S(1)} %collective-permute-done.refs_3_), channel_id=1, source_target_pairs={{0,2},{1,3},{2,0},{3,1},{4,6},{5,7},{6,4},{7,5},{8,10},{9,11},{10,... | collective-permute-start | bytes 792584 | tf_op jit(solution)/shard_map/ppermute | solution.py:266
  17.9 6.1 %collective-permute-start.3 = (bf16[1032,128]{1,0:T(8,128)(2,1)S(1)}, bf16[1032,128]{1,0:T(8,128)(2,1)S(1)}, u32[]{:S(2)}, u32[]{:S(2)}) collective-permute-start(bf16[1032,128]{1,0:T(8,128)(2,1)S(1)} %collective-permute-done.refs_3_), channel_id=1, source_target_pairs={{0,1},{1,0},{2,3},{3,2},{4,5},{5,4},{6,7},{7,6},{8,9},{9,8},{10,11... | collective-permute-start | bytes 792584 | tf_op jit(solution)/shard_map/ppermute | solution.py:266
  18.4 5.6 %collective-permute-start.4 = (bf16[1032,128]{1,0:T(8,128)(2,1)S(1)}, bf16[1032,128]{1,0:T(8,128)(2,1)S(1)}, u32[]{:S(2)}, u32[]{:S(2)}) collective-permute-start(bf16[1032,128]{1,0:T(8,128)(2,1)S(1)} %collective-permute-done.1.refs_4_), channel_id=1, source_target_pairs={{0,1},{1,0},{2,3},{3,2},{4,5},{5,4},{6,7},{7,6},{8,9},{9,8},{10,11... | collective-permute-start | bytes 792584 | tf_op jit(solution)/shard_map/ppermute | solution.py:266
  23.9 1.7 %collective-permute-start.6 = (bf16[1032,128]{1,0:T(8,128)(2,1)S(1)}, bf16[1032,128]{1,0:T(8,128)(2,1)S(1)}, u32[]{:S(2)}, u32[]{:S(2)}) collective-permute-start(bf16[1032,128]{1,0:T(8,128)(2,1)S(1)} %collective-permute-done.5.refs_7_), channel_id=1, source_target_pairs={{0,1},{1,0},{2,3},{3,2},{4,5},{5,4},{6,7},{7,6},{8,9},{9,8},{10,11... | collective-permute-start | bytes 792584 | tf_op jit(solution)/shard_map/ppermute | solution.py:266
